TPU v7x, 768 devices: a whole 4x8x12 slice. The times are simulated.
768 devices in a mesh: space: 24 (over x, z_lo), band: 32 (over z_hi, y, core).
Axes of the slice: x: 4, y: 8, z: 12 (z_hi: 2, z_lo: 6; z = z_hi * 6 + z_lo), core: 2. Of those that a mesh axis runs over, the one named last changes fastest.
Arguments:
- orbitals: float32 [768, 48, 2048], P('band', 'space'), may hold values from -6 to 6
- potential: float32 [48, 2048], P('space'), may hold values from 0 to 2
Outputs:
- filtered: float32 [768, 48, 2048], P('band', 'space')
- margin: float32 [768, 768], P('band')
All inputs are finite; a program needn't handle non-finite values.
Results may differ from a plain program's by a relative error of at most 0.0002.
Values sent between devices are 32-bit elements; how exact they have to be, the bound alone decides.
A program may use at most 32 MiB of HBM per device.

v0:
```python
import jax
import jax.numpy as jnp
from jax import lax
from jax.sharding import PartitionSpec as P

NZ = 64


def padded_2(cells, sides, width):
    for axis, dim in sides:
        count = lax.axis_size(axis)
        head = lax.slice_in_dim(cells, 0, width, axis=dim)
        tail = lax.slice_in_dim(cells, cells.shape[dim] - width, cells.shape[dim], axis=dim)
        cells = jnp.concatenate(
            [
                lax.ppermute(tail, axis, [(i, (i + 1) % count) for i in range(count)]),
                cells,
                lax.ppermute(head, axis, [((i + 1) % count, i) for i in range(count)]),
            ],
            axis=dim,
        )
    return cells


def from_everyone(shard, axis):
    size = lax.axis_size(axis)
    return lax.all_to_all(
        jnp.broadcast_to(shard[None], (size, *shard.shape)), axis, 0, 0, tiled=True
    )


def taken_together(shard, axis):
    everything = from_everyone(shard, axis)
    return jnp.sum(everything, axis=0)


def shift_plane(flat, step, depth):
    pos = lax.broadcasted_iota(jnp.int32, (flat.shape[-1],), 0) % depth
    inside = (pos + step >= 0) & (pos + step < depth)
    direct = jnp.roll(flat, -step, axis=-1)
    if step > 0:
        wrapped = jnp.roll(flat, depth - step, axis=-1)
    else:
        wrapped = jnp.roll(flat, -step - depth, axis=-1)
    return jnp.where(inside, direct, wrapped)


def plane_terms(center, depth):
    near = jnp.roll(center, -depth, axis=-1) + jnp.roll(center, depth, axis=-1)
    far = jnp.roll(center, -2 * depth, axis=-1) + jnp.roll(center, 2 * depth, axis=-1)
    near = near + shift_plane(center, 1, depth) + shift_plane(center, -1, depth)
    far = far + shift_plane(center, 2, depth) + shift_plane(center, -2, depth)
    return 4.0 / 3.0 * near - 1.0 / 12.0 * far


def apply_hamiltonian(field, potential):
    padded = padded_2(field, (("space", 1),), 2)
    center = padded[:, 2:-2]
    near = padded[:, 1:-3] + padded[:, 3:-1]
    far = padded[:, :-4] + padded[:, 4:]
    laplace = 4.0 / 3.0 * near - 1.0 / 12.0 * far + plane_terms(center, NZ) - 7.5 * center
    return -0.5 * laplace + potential[None] * center


def chebyshev(block, potential, operator):
    first = (operator(block, potential) - 6.0 * block) / 4.0
    second = 2.0 * (operator(first, potential) - 6.0 * first) / 4.0 - block
    return 2.0 * (operator(second, potential) - 6.0 * second) / 4.0 - first


def shards(orbitals, potential):
    filtered = chebyshev(orbitals, potential, apply_hamiltonian)
    orb_count = filtered.shape[0]
    layers = filtered.shape[1]
    plane = filtered.shape[2]
    flat = filtered.reshape(orb_count, layers * plane)
    regrouped = lax.all_to_all(flat, "band", split_axis=1, concat_axis=0, tiled=True)
    partial_sum = jnp.dot(
        regrouped, regrouped.T, precision=lax.Precision.HIGHEST, preferred_element_type=jnp.float32
    )
    total_cells = layers * lax.axis_size("space") * plane
    rows = lax.psum_scatter(partial_sum, "band", scatter_dimension=0, tiled=True)
    rows = taken_together(rows, "space")
    return (filtered, rows * (1.0 / total_cells))


def solution(mesh):
    return jax.shard_map(
        shards,
        mesh=mesh,
        in_specs=(P("band", "space", None), P("space", None)),
        out_specs=(P("band", "space", None), P("band", None)),
        check_vma=False,
    )
```

profile of v0, /device:TPU:1, one launch (start us, length us, event | category | flops | bytes accessed | tf_op | source)
XLA Modules:
  0.0 368.6 jit_solution(15842927216560185768)
XLA Ops:
  7.2 15.6 %collective-permute-start.1 = (f32[24,2,2048]{2,1,0:T(2,128)}, f32[24,2,2048]{2,1,0:T(2,128)S(1)}, u32[]{:S(2)}, u32[]{:S(2)}) collective-permute-start(f32[24,2,2048]{2,1,0:T(2,128)} %param.2), channel_id=1, source_target_pairs={{32,0},{64,32},{96,64},{128,96},{160,128},{192,160},{224,192},{256... | collective-permute-start | bytes 1179656 | tf_op jit(solution)/shard_map/ppermute | solution.py:18
  22.8 1.9 collective-permute-start
  26.4 0.8 fusion.82
  27.2 0.8 fusion.88
  28.1 0.8 fusion.80
  28.9 0.8 fusion.89
  29.8 1.2 fusion.85
  33.4 8.2 %collective-permute-done = f32[24,2,2048]{2,1,0:T(2,128)S(1)} collective-permute-done((f32[24,2,2048]{2,1,0:T(2,128)}, f32[24,2,2048]{2,1,0:T(2,128)S(1)}, u32[]{:S(2)}, u32[]{:S(2)}) %collective-permute-start) | collective-permute-done | bytes 393248 | tf_op jit(solution)/shard_map/ppermute | solution.py:16
  41.6 7.5 %broadcast_multiply_fusion = (f32[24,2,2048]{2,1,0:T(2,128)S(1)}, f32[24,2,2048]{2,1,0:T(2,128)S(1)}) fusion(f32[24,2,2048]{2,1,0:T(2,128)S(1)} %copy-done, f32[2,2048]{1,0:T(2,128)S(1)} %copy-done.2, f32[24,2,62]{2,1,0:T(2,128)S(1)} %get-tuple-element.73, f32[24,2,1986]{2,1,0:T(2,128)S(1)} %get-tuple-element.75, f32[24,2,2046]{2,1,0:T(2,128)S(1)} %get-tuple-element.69, ...), kind=kLoop, calls=%fused_computation.63 | loop fusion | flops 4030464 | bytes 6709248 | tf_op jit(solution)/shard_map/div | solution.py:66
  49.6 3.7 %collective-permute-start.3 = (f32[24,2,2048]{2,1,0:T(2,128)S(1)}, f32[24,2,2048]{2,1,0:T(2,128)S(1)}, u32[]{:S(2)}, u32[]{:S(2)}) collective-permute-start(f32[24,2,2048]{2,1,0:T(2,128)S(1)} %get-tuple-element.2), channel_id=1, source_target_pairs={{32,0},{64,32},{96,64},{128,96},{160,128},{192,160},{224,192},{256... | collective-permute-start | bytes 1179656 | tf_op jit(solution)/shard_map/ppermute | solution.py:18
  53.3 1.9 collective-permute-start.2
  57.8 2.5 collective-permute-done.3
  60.3 10.6 %collective-permute-done.2 = f32[24,2,2048]{2,1,0:T(2,128)S(1)} collective-permute-done((f32[24,2,2048]{2,1,0:T(2,128)S(1)}, f32[24,2,2048]{2,1,0:T(2,128)S(1)}, u32[]{:S(2)}, u32[]{:S(2)}) %collective-permute-start.2) | collective-permute-done | bytes 393248 | tf_op jit(solution)/shard_map/ppermute | solution.py:16
  71.0 7.6 %multiply_subtract_fusion.1 = f32[24,2,2048]{2,1,0:T(2,128)S(1)} fusion(f32[24,2,2048]{2,1,0:T(2,128)S(1)} %copy-done, f32[24,2,2048]{2,1,0:T(2,128)S(1)} %get-tuple-element.3, f32[24,2,62]{2,1,0:T(2,128)S(1)} %get-tuple-element.49, f32[24,2,1986]{2,1,0:T(2,128)S(1)} %get-tuple-element.51, f32[24,2,2046]{2,1,0:T(2,128)S(1)} %get-tuple-element.45, ...), kind=kLoop, calls=%fused_computation.61 | loop fusion | flops 4128768 | bytes 7102464 | tf_op jit(solution)/shard_map/sub | solution.py:67
  79.1 4.0 %collective-permute-start.5 = (f32[24,2,2048]{2,1,0:T(2,128)S(1)}, f32[24,2,2048]{2,1,0:T(2,128)S(1)}, u32[]{:S(2)}, u32[]{:S(2)}) collective-permute-start(f32[24,2,2048]{2,1,0:T(2,128)S(1)} %multiply_subtract_fusion.1), channel_id=1, source_target_pairs={{32,0},{64,32},{96,64},{128,96},{160,128},{192,160},{224,192},{256... | collective-permute-start | bytes 1179656 | tf_op jit(solution)/shard_map/ppermute | solution.py:18
  83.1 2.1 collective-permute-start.4
  87.8 1.2 collective-permute-done.5
  89.0 10.7 %collective-permute-done.4 = f32[24,2,2048]{2,1,0:T(2,128)S(1)} collective-permute-done((f32[24,2,2048]{2,1,0:T(2,128)S(1)}, f32[24,2,2048]{2,1,0:T(2,128)S(1)}, u32[]{:S(2)}, u32[]{:S(2)}) %collective-permute-start.4) | collective-permute-done | bytes 393248 | tf_op jit(solution)/shard_map/ppermute | solution.py:16
  99.8 7.7 %multiply_subtract_fusion = f32[24,2,2048]{2,1,0:T(2,128)S(1)} fusion(f32[24,2,2048]{2,1,0:T(2,128)S(1)} %multiply_subtract_fusion.1, f32[24,2,62]{2,1,0:T(2,128)S(1)} %get-tuple-element.25, f32[24,2,1986]{2,1,0:T(2,128)S(1)} %get-tuple-element.27, f32[24,2,2046]{2,1,0:T(2,128)S(1)} %get-tuple-element.21, f32[24,2,2]{2,1,0:T(2,128)S(1)} %get-tuple-element.23, ...), kind=kLoop, calls=%fused_computation.60 | loop fusion | flops 4227072 | bytes 6709248 | tf_op jit(solution)/shard_map/sub | solution.py:68
  108.0 39.1 %all_to_all.24 = f32[24,32,128]{2,0,1:T(8,128)S(1)} all-to-all(f32[24,32,128]{2,0,1:T(8,128)S(1)} %copy.6), channel_id=1, replica_groups=mesh['space'=24,'band'=32] {'band'}, dimensions={1} | all-to-all | bytes 786432 | tf_op jit(solution)/shard_map/all_to_all | solution.py:77
  147.1 3.4 fusion.91
  150.6 145.8 %reduce-scatter.2.cloned.1.call-done = f32[24,768]{1,0:T(8,128)} async-done(((f32[768,768]{1,0:T(8,128)}), f32[24,768]{1,0:T(8,128)}) %reduce-scatter.2.cloned.1.call-update) | async-done | bytes 73744 | tf_op jit(solution)/shard_map/reduce_scatter | solution.py:82
  296.4 1.0 broadcast_in_dim.50
  297.4 63.7 %all_to_all.25 = f32[24,24,768]{2,1,0:T(8,128)S(1)} all-to-all(f32[24,24,768]{2,1,0:T(8,128)S(1)} %broadcast_in_dim.50), channel_id=1, replica_groups=mesh['space'=24,'band'=32] {'space'}, dimensions={0} | all-to-all | bytes 3538944 | tf_op jit(solution)/shard_map/all_to_all | solution.py:27
  (47 shorter events, 11.5 us)
Async XLA Ops:
  7.2 23.8 %copy-start = (f32[24,2,2048]{2,1,0:T(2,128)S(1)}, f32[24,2,2048]{2,1,0:T(2,128)}, u32[]{:S(2)}) copy-start(f32[24,2,2048]{2,1,0:T(2,128)} %param.2) | copy-start | bytes 1179652
  7.2 289.2 %reduce-scatter.2.cloned.1.call-start = ((), (), s32[]{:S(2)}) async-start(), calls=%async_computation.3 | async-start | bytes 2433024 | tf_op jit(solution)/shard_map/reduce_scatter | solution.py:82
  7.2 26.2 %collective-permute-start.1 = (f32[24,2,2048]{2,1,0:T(2,128)}, f32[24,2,2048]{2,1,0:T(2,128)S(1)}, u32[]{:S(2)}, u32[]{:S(2)}) collective-permute-start(f32[24,2,2048]{2,1,0:T(2,128)} %param.2), channel_id=1, source_target_pairs={{32,0},{64,32},{96,64},{128,96},{160,128},{192,160},{224,192},{256... | collective-permute-start | bytes 1179656 | tf_op jit(solution)/shard_map/ppermute | solution.py:18
  22.8 18.7 %collective-permute-start = (f32[24,2,2048]{2,1,0:T(2,128)}, f32[24,2,2048]{2,1,0:T(2,128)S(1)}, u32[]{:S(2)}, u32[]{:S(2)}) collective-permute-start(f32[24,2,2048]{2,1,0:T(2,128)} %param.2), channel_id=1, source_target_pairs={{0,32},{32,64},{64,96},{96,128},{128,160},{160,192},{192,224},{224... | collective-permute-start | bytes 1179656 | tf_op jit(solution)/shard_map/ppermute | solution.py:16
  31.9 1.4 copy-start.2
  49.6 10.8 %collective-permute-start.3 = (f32[24,2,2048]{2,1,0:T(2,128)S(1)}, f32[24,2,2048]{2,1,0:T(2,128)S(1)}, u32[]{:S(2)}, u32[]{:S(2)}) collective-permute-start(f32[24,2,2048]{2,1,0:T(2,128)S(1)} %get-tuple-element.2), channel_id=1, source_target_pairs={{32,0},{64,32},{96,64},{128,96},{160,128},{192,160},{224,192},{256... | collective-permute-start | bytes 1179656 | tf_op jit(solution)/shard_map/ppermute | solution.py:18
  53.3 17.7 %collective-permute-start.2 = (f32[24,2,2048]{2,1,0:T(2,128)S(1)}, f32[24,2,2048]{2,1,0:T(2,128)S(1)}, u32[]{:S(2)}, u32[]{:S(2)}) collective-permute-start(f32[24,2,2048]{2,1,0:T(2,128)S(1)} %get-tuple-element.2), channel_id=1, source_target_pairs={{0,32},{32,64},{64,96},{96,128},{128,160},{160,192},{192,224},{224... | collective-permute-start | bytes 1179656 | tf_op jit(solution)/shard_map/ppermute | solution.py:16
  79.1 9.9 %collective-permute-start.5 = (f32[24,2,2048]{2,1,0:T(2,128)S(1)}, f32[24,2,2048]{2,1,0:T(2,128)S(1)}, u32[]{:S(2)}, u32[]{:S(2)}) collective-permute-start(f32[24,2,2048]{2,1,0:T(2,128)S(1)} %multiply_subtract_fusion.1), channel_id=1, source_target_pairs={{32,0},{64,32},{96,64},{128,96},{160,128},{192,160},{224,192},{256... | collective-permute-start | bytes 1179656 | tf_op jit(solution)/shard_map/ppermute | solution.py:18
  83.1 16.6 %collective-permute-start.4 = (f32[24,2,2048]{2,1,0:T(2,128)S(1)}, f32[24,2,2048]{2,1,0:T(2,128)S(1)}, u32[]{:S(2)}, u32[]{:S(2)}) collective-permute-start(f32[24,2,2048]{2,1,0:T(2,128)S(1)} %multiply_subtract_fusion.1), channel_id=1, source_target_pairs={{0,32},{32,64},{64,96},{96,128},{128,160},{160,192},{192,224},{224... | collective-permute-start | bytes 1179656 | tf_op jit(solution)/shard_map/ppermute | solution.py:16
  107.4 43.1 %copy-start.1 = (f32[24,2,2048]{2,1,0:T(2,128)}, f32[24,2,2048]{2,1,0:T(2,128)S(1)}, u32[]{:S(2)}) copy-start(f32[24,2,2048]{2,1,0:T(2,128)S(1)} %multiply_subtract_fusion) | copy-start | bytes 1179652
Sparse Core Ops, SparseCore 0:
  150.7 145.6 reduce-scatter.1
where the time goes:
time: 372 us; the launch traced here: 369 us
  waiting for transfers between devices  179 us (48%)
  blocking collectives  103 us (28%)
  starting transfers between devices  29.3 us (8%)
  other arithmetic  23.6 us (6%)
  local copies, waits for them, and re-layouts  16.2 us (4%)
  between operations  14.3 us (4%)
    reduce_scatter x1, waiting for transfers between devices, shards(): lax.psum_scatter(partial_sum, 'band', scatter_dimension=0, tiled=True)  146 us
    all_to_all x1, blocking collectives, from_everyone(): lax.all_to_all(jnp.broadcast_to(shard[None], (size, *shard.shape)), axis,...  63.7 us
    all_to_all x1, blocking collectives, shards(): lax.all_to_all(flat, 'band', split_axis=1, concat_axis=0, tiled=True)  39.1 us
    ppermute x3, waiting for transfers between devices, padded_2(): lax.ppermute(tail, axis, [(i, (i + 1) % count) for i in range(count)])  29.5 us
    ppermute x3, starting transfers between devices, padded_2(): lax.ppermute(head, axis, [((i + 1) % count, i) for i in range(count)])  23.3 us
    sub x1, other arithmetic, chebyshev(): return 2.0 * (operator(second, potential) - 6.0 * second) / 4.0 - first  7.67 us
    sub x1, other arithmetic, chebyshev(): second = 2.0 * (operator(first, potential) - 6.0 * first) / 4.0 - block  7.64 us
    div x1, other arithmetic, chebyshev(): first = (operator(block, potential) - 6.0 * block) / 4.0  7.52 us
  transfers between devices with their start and end apart: 7, of which 6 were waited for; matrix products, arithmetic and copies ran while one was open for 4% of the time, Pallas kernels for 0%

commit v1 on v0

--- a/solution.py
+++ b/solution.py
@@ -1,7 +1,286 @@
 import jax
 import jax.numpy as jnp
 from jax import lax
+from jax.experimental import pallas as pl
+from jax.experimental.pallas import tpu as pltpu
 from jax.sharding import PartitionSpec as P
+
+MESH = pl.DeviceIdType.MESH
+NX_CHIPS, NZ_LO, NZ_HI, N_Y = 4, 6, 2, 8
+N_Z = NZ_LO * NZ_HI
+ROWS = 24
+ORBS = 768
+LANES = 128
+TILES = ORBS // LANES
+CELLS = 48 * 2048
+
+
+def where_am_i():
+    space, band = lax.axis_index("space"), lax.axis_index("band")
+    x, z_lo = lax.div(space, NZ_LO), lax.rem(space, NZ_LO)
+    core, pair = lax.rem(band, 2), lax.div(band, 2)
+    y, z_hi = lax.rem(pair, N_Y), lax.div(pair, N_Y)
+    return x, y, z_hi * NZ_LO + z_lo, core
+
+
+def device(x, y, z, core):
+    z_hi, z_lo = lax.div(z, NZ_LO), lax.rem(z, NZ_LO)
+    return (x * NZ_LO + z_lo, (z_hi * N_Y + y) * 2 + core)
+
+
+def margin_kernel(
+    cells_ref, out_ref, held, rows, cat, part, ring, mine, pieces,
+    meet_send, meet_recv, core_send, core_recv, ring_send, ring_recv,
+    piece_send, piece_recv, out_send, out_recv,
+):
+    x, y, z, core = where_am_i()
+    z_hi, z_lo = lax.div(z, NZ_LO), lax.rem(z, NZ_LO)
+    band = (z_hi * N_Y + y) * 2 + core
+    other = device(x, y, z, 1 - core)
+    up = device(x, lax.rem(y + 1, N_Y), z, core)
+    down = device(x, lax.rem(y + N_Y - 1, N_Y), z, core)
+    half_z = NZ_LO // 2
+    above, below = lax.rem(z + half_z, N_Z), lax.rem(z + N_Z - half_z, N_Z)
+    spot = z_hi * 24 + x * NZ_LO + z_lo
+
+    def spot_device(index):
+        hi, rest = lax.div(index, 24), lax.rem(index, 24)
+        return (rest, (hi * N_Y + y) * 2 + core)
+
+    barrier = pltpu.get_barrier_semaphore()
+
+    def greet(peer):
+        pl.semaphore_signal(barrier, inc=1, device_id=peer, device_id_type=MESH)
+
+    for peer in (other, up, down):
+        greet(peer)
+
+    def greet_meeting(k, carry):
+        greet(device(x, k, above, core))
+        greet(device(x, k, below, core))
+        return carry
+
+    lax.fori_loop(0, N_Y, greet_meeting, 0)
+
+    def greet_spots(k, carry):
+        greet(spot_device(lax.rem(spot + k, 48)))
+        return carry
+
+    lax.fori_loop(1, 48, greet_spots, 0)
+    pl.semaphore_wait(barrier, 3 + 2 * N_Y + 47)
+
+    def meeting(k, way):
+        to_y = lax.rem(y + k, N_Y)
+        to_z, plane = (above, z_hi) if way == 0 else (below, 1 - z_hi)
+        return pltpu.make_async_remote_copy(
+            src_ref=cells_ref.at[pl.ds(16 * plane + 2 * to_y, 2)],
+            dst_ref=held.at[:, pl.ds(pl.multiple_of(ROWS * band, 8), ROWS), :],
+            send_sem=meet_send.at[way, k],
+            recv_sem=meet_recv.at[z_hi * N_Y + y],
+            device_id=device(x, to_y, to_z, core),
+            device_id_type=MESH,
+        )
+
+    def start_meeting(k, carry):
+        meeting(k, 0).start()
+        meeting(k, 1).start()
+        return carry
+
+    lax.fori_loop(0, N_Y, start_meeting, 0)
+
+    def across(j):
+        place = held.at[:, pl.ds(pl.multiple_of(ROWS * (2 * j + core), 8), ROWS), :]
+        return pltpu.make_async_remote_copy(
+            src_ref=place, dst_ref=place,
+            send_sem=core_send.at[j], recv_sem=core_recv.at[j],
+            device_id=other, device_id_type=MESH,
+        )
+
+    def arrived(k, carry):
+        for hi in range(2):
+            j = hi * N_Y + lax.rem(y + k, N_Y)
+            place = held.at[:, pl.ds(pl.multiple_of(ROWS * (2 * j + core), 8), ROWS), :]
+            pltpu.make_async_remote_copy(
+                src_ref=place, dst_ref=place,
+                send_sem=core_send.at[j], recv_sem=meet_recv.at[j],
+                device_id=other, device_id_type=MESH,
+            ).wait_recv()
+            across(j).start()
+        return carry
+
+    lax.fori_loop(0, N_Y, arrived, 0)
+
+    def crossed(j, carry):
+        across(j).wait_recv()
+        return carry
+
+    lax.fori_loop(0, 2 * N_Y, crossed, 0)
+
+    for g in range(2 * N_Y):
+        for k in range(2):
+            rows[g, :, LANES * k:LANES * (k + 1)] = held[
+                k, pl.ds(pl.multiple_of(ROWS * (2 * g + core), 8), ROWS), :
+            ]
+    left = rows[...].reshape(2 * N_Y * ROWS, 2 * LANES)
+    left_hi = left.astype(jnp.bfloat16)
+    left_lo = (left - left_hi.astype(jnp.float32)).astype(jnp.bfloat16)
+    left_cat = jnp.concatenate([left_hi, left_hi, left_lo], axis=1)
+    for k in range(2):
+        plane = held[k]
+        hi = plane.astype(jnp.bfloat16)
+        lo = (plane - hi.astype(jnp.float32)).astype(jnp.bfloat16)
+        for slot, value in enumerate((hi, lo, hi)):
+            cat[:, 2 * LANES * slot + LANES * k:2 * LANES * slot + LANES * (k + 1)] = value
+    for n in range(3):
+        block = lax.dot_general(
+            left_cat, cat[256 * n:256 * (n + 1), :], (((1,), (1,)), ((), ())),
+            preferred_element_type=jnp.float32,
+        )
+        part[:, :, :, 256 * n:256 * (n + 1)] = block.reshape(2, N_Y, ROWS, 256)
+
+    def hop(way, step, h, source):
+        return pltpu.make_async_remote_copy(
+            src_ref=source,
+            dst_ref=ring.at[way, step, h],
+            send_sem=ring_send.at[way, step, h],
+            recv_sem=ring_recv.at[way, step, h],
+            device_id=up if way == 0 else down,
+            device_id_type=MESH,
+        )
+
+    def goal(way, step):
+        return lax.rem(y + (4 - step if way == 0 else N_Y - 4 + step), N_Y)
+
+    for way in range(2):
+        hop(way, 0, way, part.at[way, goal(way, 0)]).start()
+    for way in range(2):
+        hop(way, 1, 1 - way, part.at[1 - way, goal(way, 1)]).start()
+    for step in range(4):
+        for first in range(2):
+            for way in range(2):
+                h = way if (first == 1) == (step != 0) else 1 - way
+                if step == 0 and first == 1:
+                    continue
+                if step == 0:
+                    h = way
+                slot = ring.at[way, step, h]
+                hop(way, step, h, slot).wait_recv()
+                if step < 3:
+                    ring[way, step, h] = ring[way, step, h] + part[h, goal(way, step + 1)]
+                    hop(way, step + 1, h, slot).start()
+
+    for h in range(2):
+        total = part[h, y] + ring[0, 3, h] + ring[1, 3, h]
+        for t in range(TILES):
+            mine[ROWS * h:ROWS * (h + 1), t, :] = total[:, LANES * t:LANES * (t + 1)]
+
+    def piece(k):
+        peer = lax.rem(spot + k, 48)
+        return pltpu.make_async_remote_copy(
+            src_ref=mine.at[peer], dst_ref=pieces.at[spot],
+            send_sem=piece_send.at[k], recv_sem=piece_recv.at[spot],
+            device_id=spot_device(peer), device_id_type=MESH,
+        )
+
+    def start_piece(k, carry):
+        piece(k).start()
+        return carry
+
+    lax.fori_loop(1, 48, start_piece, 0)
+    pieces[spot] = mine[spot]
+
+    def wait_piece(k, carry):
+        source = lax.rem(spot + k, 48)
+        pltpu.make_async_remote_copy(
+            src_ref=mine.at[source], dst_ref=pieces.at[source],
+            send_sem=piece_send.at[k], recv_sem=piece_recv.at[source],
+            device_id=spot_device(source), device_id_type=MESH,
+        ).wait_recv()
+        return carry
+
+    lax.fori_loop(1, 48, wait_piece, 0)
+    row = lax.rem(spot, 24)
+    out_ref[row] = jnp.sum(pieces[...], axis=0) * (1.0 / CELLS)
+
+    def give(k):
+        peer = lax.rem(row + k, 24)
+        return pltpu.make_async_remote_copy(
+            src_ref=out_ref.at[row], dst_ref=out_ref.at[row],
+            send_sem=out_send.at[k], recv_sem=out_recv.at[row],
+            device_id=(peer, band), device_id_type=MESH,
+        )
+
+    def start_give(k, carry):
+        give(k).start()
+        return carry
+
+    lax.fori_loop(1, 24, start_give, 0)
+
+    def wait_give(k, carry):
+        source = lax.rem(row + k, 24)
+        pltpu.make_async_remote_copy(
+            src_ref=out_ref.at[source], dst_ref=out_ref.at[source],
+            send_sem=out_send.at[k], recv_sem=out_recv.at[source],
+            device_id=(source, band), device_id_type=MESH,
+        ).wait_recv()
+        return carry
+
+    lax.fori_loop(1, 24, wait_give, 0)
+
+    def sent_meeting(k, carry):
+        meeting(k, 0).wait_send()
+        meeting(k, 1).wait_send()
+        return carry
+
+    lax.fori_loop(0, N_Y, sent_meeting, 0)
+
+    def sent_across(j, carry):
+        across(j).wait_send()
+        return carry
+
+    lax.fori_loop(0, 2 * N_Y, sent_across, 0)
+    for way in range(2):
+        for step in range(4):
+            for h in range(2):
+                if step > 0 or h == way:
+                    hop(way, step, h, ring.at[way, step, h]).wait_send()
+
+    def sent_piece(k, carry):
+        piece(k).wait_send()
+        return carry
+
+    lax.fori_loop(1, 48, sent_piece, 0)
+
+    def sent_give(k, carry):
+        give(k).wait_send()
+        return carry
+
+    lax.fori_loop(1, 24, sent_give, 0)
+
+
+def margin_of(filtered):
+    cells = filtered.reshape(ROWS, 32, LANES).transpose(1, 0, 2)
+    dma = pltpu.SemaphoreType.DMA
+    out = pl.pallas_call(
+        margin_kernel,
+        out_shape=jax.ShapeDtypeStruct((ROWS, TILES, LANES), jnp.float32),
+        in_specs=[pl.BlockSpec(memory_space=pltpu.VMEM)],
+        out_specs=pl.BlockSpec(memory_space=pltpu.VMEM),
+        scratch_shapes=[
+            pltpu.VMEM((2, ORBS, LANES), jnp.float32),
+            pltpu.VMEM((2 * N_Y, ROWS, 2 * LANES), jnp.float32),
+            pltpu.VMEM((ORBS, 6 * LANES), jnp.bfloat16),
+            pltpu.VMEM((2, N_Y, ROWS, ORBS), jnp.float32),
+            pltpu.VMEM((2, 4, 2, ROWS, ORBS), jnp.float32),
+            pltpu.VMEM((48, TILES, LANES), jnp.float32),
+            pltpu.VMEM((48, TILES, LANES), jnp.float32),
+            dma((2, N_Y)), dma((2 * N_Y,)), dma((2 * N_Y,)), dma((2 * N_Y,)),
+            dma((2, 4, 2)), dma((2, 4, 2)), dma((48,)), dma((48,)), dma((24,)), dma((24,)),
+        ],
+        compiler_params=pltpu.CompilerParams(collective_id=0, has_side_effects=True),
+    )(cells)
+    return out.reshape(ROWS, ORBS)
+
 
 NZ = 64
 
@@ -22,18 +301,6 @@
     return cells
 
 
-def from_everyone(shard, axis):
-    size = lax.axis_size(axis)
-    return lax.all_to_all(
-        jnp.broadcast_to(shard[None], (size, *shard.shape)), axis, 0, 0, tiled=True
-    )
-
-
-def taken_together(shard, axis):
-    everything = from_everyone(shard, axis)
-    return jnp.sum(everything, axis=0)
-
-
 def shift_plane(flat, step, depth):
     pos = lax.broadcasted_iota(jnp.int32, (flat.shape[-1],), 0) % depth
     inside = (pos + step >= 0) & (pos + step < depth)
@@ -70,18 +337,7 @@
 
 def shards(orbitals, potential):
     filtered = chebyshev(orbitals, potential, apply_hamiltonian)
-    orb_count = filtered.shape[0]
-    layers = filtered.shape[1]
-    plane = filtered.shape[2]
-    flat = filtered.reshape(orb_count, layers * plane)
-    regrouped = lax.all_to_all(flat, "band", split_axis=1, concat_axis=0, tiled=True)
-    partial_sum = jnp.dot(
-        regrouped, regrouped.T, precision=lax.Precision.HIGHEST, preferred_element_type=jnp.float32
-    )
-    total_cells = layers * lax.axis_size("space") * plane
-    rows = lax.psum_scatter(partial_sum, "band", scatter_dimension=0, tiled=True)
-    rows = taken_together(rows, "space")
-    return (filtered, rows * (1.0 / total_cells))
+    return (filtered, margin_of(filtered))
 
 
 def solution(mesh):

time: 372 us -> 180 us (0.48)
  waiting for transfers between devices: 179 us -> 35.5 us
  blocking collectives: 103 us -> 0 us
  Pallas kernels: 0 us -> 73.2 us
  between operations: 14.3 us -> 0.87 us
    reduce_scatter x1 -> x0, waiting for transfers between devices: 146 us -> none  [shards(): lax.psum_scatter(partial_sum, 'band', scatter_dimension=0, tiled=True)]
    all_to_all x2 -> x0, blocking collectives: 103 us -> none  [the longest x1 63.7 us: from_everyone(): lax.all_to_all(jnp.broadcast_to(shard[None], (size, *shard.shape)), axis,...]
    pallas_call x0 -> x1, Pallas kernels: none -> 73.2 us  [margin_of(): pl.pallas_call(margin_kernel, out_shape=jax.ShapeDtypeStruct((ROWS, TILES...]
  transfers between devices with their start and end apart: 7 -> 6, of which waited for: 6 -> 5; matrix products, arithmetic and copies ran while one was open for 4% -> 6% of each run, Pallas kernels for 0% -> 0%
where the time goes in v1:
time: 180 us; the launch traced here: 177 us
  Pallas kernels  73.2 us (41%)
  waiting for transfers between devices  35.5 us (20%)
  starting transfers between devices  29.2 us (16%)
  other arithmetic  22.9 us (13%)
  local copies, waits for them, and re-layouts  15.7 us (9%)
    pallas_call x1, Pallas kernels, margin_of(): pl.pallas_call(margin_kernel, out_shape=jax.ShapeDtypeStruct((ROWS, TILES...  73.2 us
    ppermute x3, waiting for transfers between devices, padded_2(): lax.ppermute(tail, axis, [(i, (i + 1) % count) for i in range(count)])  31.8 us
    ppermute x3, starting transfers between devices, padded_2(): lax.ppermute(head, axis, [((i + 1) % count, i) for i in range(count)])  23.3 us
    sub x1, other arithmetic, chebyshev(): return 2.0 * (operator(second, potential) - 6.0 * second) / 4.0 - first  7.67 us
    sub x1, other arithmetic, chebyshev(): second = 2.0 * (operator(first, potential) - 6.0 * first) / 4.0 - block  7.64 us
    div x1, other arithmetic, chebyshev(): first = (operator(block, potential) - 6.0 * block) / 4.0  7.53 us
    ppermute x3, starting transfers between devices, padded_2(): lax.ppermute(tail, axis, [(i, (i + 1) % count) for i in range(count)])  5.94 us
    slice x12, local copies, waits for them, and re-layouts, shift_plane(): direct = jnp.roll(flat, -step, axis=-1)  4.92 us
  transfers between devices with their start and end apart: 6, of which 5 were waited for; matrix products, arithmetic and copies ran while one was open for 6% of the time, Pallas kernels for 0%

profile of v1, /device:TPU:1, one launch (start us, length us, event | category | flops | bytes accessed | tf_op | source)
XLA Modules:
  0.0 177.3 jit_solution(4417816813888428658)
XLA Ops:
  0.6 15.6 %collective-permute-start.1 = (f32[24,2,2048]{2,1,0:T(2,128)}, f32[24,2,2048]{2,1,0:T(2,128)S(1)}, u32[]{:S(2)}, u32[]{:S(2)}) collective-permute-start(f32[24,2,2048]{2,1,0:T(2,128)} %param.2), channel_id=1, source_target_pairs={{32,0},{64,32},{96,64},{128,96},{160,128},{192,160},{224,192},{256... | collective-permute-start | bytes 1179656 | tf_op jit(solution)/shard_map/ppermute | solution.py:297
  16.2 1.9 %collective-permute-start = (f32[24,2,2048]{2,1,0:T(2,128)}, f32[24,2,2048]{2,1,0:T(2,128)S(1)}, u32[]{:S(2)}, u32[]{:S(2)}) collective-permute-start(f32[24,2,2048]{2,1,0:T(2,128)} %param.2), channel_id=1, source_target_pairs={{0,32},{32,64},{64,96},{96,128},{128,160},{160,192},{192,224},{224... | collective-permute-start | bytes 1179656 | tf_op jit(solution)/shard_map/ppermute | solution.py:295
  18.2 0.8 fusion.86
  19.0 0.8 fusion.83
  19.8 0.8 fusion.82
  20.7 0.8 fusion.88
  22.4 0.5 fusion.81
  22.9 0.5 fusion.87
  24.6 10.4 %collective-permute-done = f32[24,2,2048]{2,1,0:T(2,128)S(1)} collective-permute-done((f32[24,2,2048]{2,1,0:T(2,128)}, f32[24,2,2048]{2,1,0:T(2,128)S(1)}, u32[]{:S(2)}, u32[]{:S(2)}) %collective-permute-start) | collective-permute-done | bytes 393248 | tf_op jit(solution)/shard_map/ppermute | solution.py:295
  35.0 7.5 %broadcast_multiply_fusion = (f32[24,2,2048]{2,1,0:T(2,128)S(1)}, f32[24,2,2048]{2,1,0:T(2,128)S(1)}) fusion(f32[24,2,2048]{2,1,0:T(2,128)S(1)} %copy-done, f32[2,2048]{1,0:T(2,128)S(1)} %copy-done.2, f32[24,2,62]{2,1,0:T(2,128)S(1)} %get-tuple-element.73, f32[24,2,1986]{2,1,0:T(2,128)S(1)} %get-tuple-element.75, f32[24,2,2046]{2,1,0:T(2,128)S(1)} %get-tuple-element.69, ...), kind=kLoop, calls=%fused_computation.64 | loop fusion | flops 4030464 | bytes 6709248 | tf_op jit(solution)/shard_map/div | solution.py:333
  43.0 3.7 %collective-permute-start.3 = (f32[24,2,2048]{2,1,0:T(2,128)S(1)}, f32[24,2,2048]{2,1,0:T(2,128)S(1)}, u32[]{:S(2)}, u32[]{:S(2)}) collective-permute-start(f32[24,2,2048]{2,1,0:T(2,128)S(1)} %get-tuple-element.2), channel_id=1, source_target_pairs={{32,0},{64,32},{96,64},{128,96},{160,128},{192,160},{224,192},{256... | collective-permute-start | bytes 1179656 | tf_op jit(solution)/shard_map/ppermute | solution.py:297
  46.7 1.9 %collective-permute-start.2 = (f32[24,2,2048]{2,1,0:T(2,128)S(1)}, f32[24,2,2048]{2,1,0:T(2,128)S(1)}, u32[]{:S(2)}, u32[]{:S(2)}) collective-permute-start(f32[24,2,2048]{2,1,0:T(2,128)S(1)} %get-tuple-element.2), channel_id=1, source_target_pairs={{0,32},{32,64},{64,96},{96,128},{128,160},{160,192},{192,224},{224... | collective-permute-start | bytes 1179656 | tf_op jit(solution)/shard_map/ppermute | solution.py:295
  50.8 0.5 fusion.78
  51.3 2.5 %collective-permute-done.3 = f32[24,2,2048]{2,1,0:T(2,128)S(1)} collective-permute-done((f32[24,2,2048]{2,1,0:T(2,128)S(1)}, f32[24,2,2048]{2,1,0:T(2,128)S(1)}, u32[]{:S(2)}, u32[]{:S(2)}) %collective-permute-start.3) | collective-permute-done | bytes 393248 | tf_op jit(solution)/shard_map/ppermute | solution.py:297
  53.8 10.6 %collective-permute-done.2 = f32[24,2,2048]{2,1,0:T(2,128)S(1)} collective-permute-done((f32[24,2,2048]{2,1,0:T(2,128)S(1)}, f32[24,2,2048]{2,1,0:T(2,128)S(1)}, u32[]{:S(2)}, u32[]{:S(2)}) %collective-permute-start.2) | collective-permute-done | bytes 393248 | tf_op jit(solution)/shard_map/ppermute | solution.py:295
  64.4 7.6 %multiply_subtract_fusion.1 = f32[24,2,2048]{2,1,0:T(2,128)S(1)} fusion(f32[24,2,2048]{2,1,0:T(2,128)S(1)} %copy-done, f32[24,2,2048]{2,1,0:T(2,128)S(1)} %get-tuple-element.3, f32[24,2,62]{2,1,0:T(2,128)S(1)} %get-tuple-element.49, f32[24,2,1986]{2,1,0:T(2,128)S(1)} %get-tuple-element.51, f32[24,2,2046]{2,1,0:T(2,128)S(1)} %get-tuple-element.45, ...), kind=kLoop, calls=%fused_computation.62 | loop fusion | flops 4128768 | bytes 7102464 | tf_op jit(solution)/shard_map/sub | solution.py:334
  72.6 4.0 %collective-permute-start.5 = (f32[24,2,2048]{2,1,0:T(2,128)S(1)}, f32[24,2,2048]{2,1,0:T(2,128)S(1)}, u32[]{:S(2)}, u32[]{:S(2)}) collective-permute-start(f32[24,2,2048]{2,1,0:T(2,128)S(1)} %multiply_subtract_fusion.1), channel_id=1, source_target_pairs={{32,0},{64,32},{96,64},{128,96},{160,128},{192,160},{224,192},{256... | collective-permute-start | bytes 1179656 | tf_op jit(solution)/shard_map/ppermute | solution.py:297
  76.6 2.1 %collective-permute-start.4 = (f32[24,2,2048]{2,1,0:T(2,128)S(1)}, f32[24,2,2048]{2,1,0:T(2,128)S(1)}, u32[]{:S(2)}, u32[]{:S(2)}) collective-permute-start(f32[24,2,2048]{2,1,0:T(2,128)S(1)} %multiply_subtract_fusion.1), channel_id=1, source_target_pairs={{0,32},{32,64},{64,96},{96,128},{128,160},{160,192},{192,224},{224... | collective-permute-start | bytes 1179656 | tf_op jit(solution)/shard_map/ppermute | solution.py:295
  81.3 1.2 collective-permute-done.5
  82.5 10.7 %collective-permute-done.4 = f32[24,2,2048]{2,1,0:T(2,128)S(1)} collective-permute-done((f32[24,2,2048]{2,1,0:T(2,128)S(1)}, f32[24,2,2048]{2,1,0:T(2,128)S(1)}, u32[]{:S(2)}, u32[]{:S(2)}) %collective-permute-start.4) | collective-permute-done | bytes 393248 | tf_op jit(solution)/shard_map/ppermute | solution.py:295
  93.2 7.7 %multiply_subtract_fusion = f32[24,2,2048]{2,1,0:T(2,128)S(1)} fusion(f32[24,2,2048]{2,1,0:T(2,128)S(1)} %multiply_subtract_fusion.1, f32[24,2,62]{2,1,0:T(2,128)S(1)} %get-tuple-element.25, f32[24,2,1986]{2,1,0:T(2,128)S(1)} %get-tuple-element.27, f32[24,2,2046]{2,1,0:T(2,128)S(1)} %get-tuple-element.21, f32[24,2,2]{2,1,0:T(2,128)S(1)} %get-tuple-element.23, ...), kind=kLoop, calls=%fused_computation.61 | loop fusion | flops 4227072 | bytes 6709248 | tf_op jit(solution)/shard_map/sub | solution.py:335
  101.6 1.0 copy.8
  102.6 73.2 %shard_map.41 = f32[24,6,128]{2,1,0:T(8,128)} custom-call(f32[32,24,128]{2,1,0:T(8,128)} %bitcast.7), custom_call_target="tpu_custom_call" | custom-call | tf_op jit(solution)/shard_map/pallas_call | solution.py:264
  175.8 1.5 copy.9
  (40 shorter events, 8.5 us)
Async XLA Ops:
  0.6 20.9 %copy-start = (f32[24,2,2048]{2,1,0:T(2,128)S(1)}, f32[24,2,2048]{2,1,0:T(2,128)}, u32[]{:S(2)}) copy-start(f32[24,2,2048]{2,1,0:T(2,128)} %param.2) | copy-start | bytes 1179652
  0.6 23.9 %collective-permute-start.1 = (f32[24,2,2048]{2,1,0:T(2,128)}, f32[24,2,2048]{2,1,0:T(2,128)S(1)}, u32[]{:S(2)}, u32[]{:S(2)}) collective-permute-start(f32[24,2,2048]{2,1,0:T(2,128)} %param.2), channel_id=1, source_target_pairs={{32,0},{64,32},{96,64},{128,96},{160,128},{192,160},{224,192},{256... | collective-permute-start | bytes 1179656 | tf_op jit(solution)/shard_map/ppermute | solution.py:297
  16.2 18.7 %collective-permute-start = (f32[24,2,2048]{2,1,0:T(2,128)}, f32[24,2,2048]{2,1,0:T(2,128)S(1)}, u32[]{:S(2)}, u32[]{:S(2)}) collective-permute-start(f32[24,2,2048]{2,1,0:T(2,128)} %param.2), channel_id=1, source_target_pairs={{0,32},{32,64},{64,96},{96,128},{128,160},{160,192},{192,224},{224... | collective-permute-start | bytes 1179656 | tf_op jit(solution)/shard_map/ppermute | solution.py:295
  23.8 0.7 copy-start.2
  43.0 10.8 %collective-permute-start.3 = (f32[24,2,2048]{2,1,0:T(2,128)S(1)}, f32[24,2,2048]{2,1,0:T(2,128)S(1)}, u32[]{:S(2)}, u32[]{:S(2)}) collective-permute-start(f32[24,2,2048]{2,1,0:T(2,128)S(1)} %get-tuple-element.2), channel_id=1, source_target_pairs={{32,0},{64,32},{96,64},{128,96},{160,128},{192,160},{224,192},{256... | collective-permute-start | bytes 1179656 | tf_op jit(solution)/shard_map/ppermute | solution.py:297
  46.7 17.7 %collective-permute-start.2 = (f32[24,2,2048]{2,1,0:T(2,128)S(1)}, f32[24,2,2048]{2,1,0:T(2,128)S(1)}, u32[]{:S(2)}, u32[]{:S(2)}) collective-permute-start(f32[24,2,2048]{2,1,0:T(2,128)S(1)} %get-tuple-element.2), channel_id=1, source_target_pairs={{0,32},{32,64},{64,96},{96,128},{128,160},{160,192},{192,224},{224... | collective-permute-start | bytes 1179656 | tf_op jit(solution)/shard_map/ppermute | solution.py:295
  72.6 9.9 %collective-permute-start.5 = (f32[24,2,2048]{2,1,0:T(2,128)S(1)}, f32[24,2,2048]{2,1,0:T(2,128)S(1)}, u32[]{:S(2)}, u32[]{:S(2)}) collective-permute-start(f32[24,2,2048]{2,1,0:T(2,128)S(1)} %multiply_subtract_fusion.1), channel_id=1, source_target_pairs={{32,0},{64,32},{96,64},{128,96},{160,128},{192,160},{224,192},{256... | collective-permute-start | bytes 1179656 | tf_op jit(solution)/shard_map/ppermute | solution.py:297
  76.6 16.6 %collective-permute-start.4 = (f32[24,2,2048]{2,1,0:T(2,128)S(1)}, f32[24,2,2048]{2,1,0:T(2,128)S(1)}, u32[]{:S(2)}, u32[]{:S(2)}) collective-permute-start(f32[24,2,2048]{2,1,0:T(2,128)S(1)} %multiply_subtract_fusion.1), channel_id=1, source_target_pairs={{0,32},{32,64},{64,96},{96,128},{128,160},{160,192},{192,224},{224... | collective-permute-start | bytes 1179656 | tf_op jit(solution)/shard_map/ppermute | solution.py:295
  100.9 0.7 copy-start.1

commit v2 on v1

--- a/solution.py
+++ b/solution.py
@@ -8,6 +8,7 @@
 MESH = pl.DeviceIdType.MESH
 NX_CHIPS, NZ_LO, NZ_HI, N_Y = 4, 6, 2, 8
 N_Z = NZ_LO * NZ_HI
+NZ = 64
 ROWS = 24
 ORBS = 768
 LANES = 128
@@ -282,61 +283,192 @@
     return out.reshape(ROWS, ORBS)
 
 
-NZ = 64
-
-
-def padded_2(cells, sides, width):
-    for axis, dim in sides:
-        count = lax.axis_size(axis)
-        head = lax.slice_in_dim(cells, 0, width, axis=dim)
-        tail = lax.slice_in_dim(cells, cells.shape[dim] - width, cells.shape[dim], axis=dim)
-        cells = jnp.concatenate(
-            [
-                lax.ppermute(tail, axis, [(i, (i + 1) % count) for i in range(count)]),
-                cells,
-                lax.ppermute(head, axis, [((i + 1) % count, i) for i in range(count)]),
-            ],
-            axis=dim,
-        )
-    return cells
-
-
-def shift_plane(flat, step, depth):
-    pos = lax.broadcasted_iota(jnp.int32, (flat.shape[-1],), 0) % depth
-    inside = (pos + step >= 0) & (pos + step < depth)
-    direct = jnp.roll(flat, -step, axis=-1)
-    if step > 0:
-        wrapped = jnp.roll(flat, depth - step, axis=-1)
-    else:
-        wrapped = jnp.roll(flat, -step - depth, axis=-1)
-    return jnp.where(inside, direct, wrapped)
-
-
-def plane_terms(center, depth):
-    near = jnp.roll(center, -depth, axis=-1) + jnp.roll(center, depth, axis=-1)
-    far = jnp.roll(center, -2 * depth, axis=-1) + jnp.roll(center, 2 * depth, axis=-1)
-    near = near + shift_plane(center, 1, depth) + shift_plane(center, -1, depth)
-    far = far + shift_plane(center, 2, depth) + shift_plane(center, -2, depth)
-    return 4.0 / 3.0 * near - 1.0 / 12.0 * far
-
-
-def apply_hamiltonian(field, potential):
-    padded = padded_2(field, (("space", 1),), 2)
-    center = padded[:, 2:-2]
-    near = padded[:, 1:-3] + padded[:, 3:-1]
-    far = padded[:, :-4] + padded[:, 4:]
-    laplace = 4.0 / 3.0 * near - 1.0 / 12.0 * far + plane_terms(center, NZ) - 7.5 * center
-    return -0.5 * laplace + potential[None] * center
-
-
-def chebyshev(block, potential, operator):
-    first = (operator(block, potential) - 6.0 * block) / 4.0
-    second = 2.0 * (operator(first, potential) - 6.0 * first) / 4.0 - block
-    return 2.0 * (operator(second, potential) - 6.0 * second) / 4.0 - first
+def filter_kernel(
+    orbs_ref, pot_ref, home_ref, field, first, second, last, pot,
+    in_send, in_recv, pot_send, pot_recv, share_send, share_recv, back_send, back_recv,
+):
+    x, y, z, core = where_am_i()
+    z_hi, z_lo = lax.div(z, NZ_LO), lax.rem(z, NZ_LO)
+    band = (z_hi * N_Y + y) * 2 + core
+    me = x * NZ_LO + z_lo
+    quarter = lax.rem(y, 2) * 2 + core
+    tile = lax.rem(quarter, 2)
+    plane = lax.div(quarter, 2)
+
+    def friend(k):
+        q = lax.rem(quarter + k, 4)
+        return q, (me, (z_hi * N_Y + lax.div(y, 2) * 2 + lax.div(q, 2)) * 2 + lax.rem(q, 2))
+
+    barrier = pltpu.get_barrier_semaphore()
+
+    def greet(k, carry):
+        pl.semaphore_signal(
+            barrier, inc=1, device_id=(lax.rem(me + k, 24), band), device_id_type=MESH
+        )
+        return carry
+
+    lax.fori_loop(1, 24, greet, 0)
+    for k in range(1, 4):
+        pl.semaphore_signal(barrier, inc=1, device_id=friend(k)[1], device_id_type=MESH)
+    pl.semaphore_wait(barrier, 26)
+
+    def pot_piece(source, q):
+        return pot.at[2 * source + lax.div(q, 2), pl.ds(pl.multiple_of(8 * lax.rem(q, 2), 8), 8)]
+
+    def pot_copy(k, source):
+        return pltpu.make_async_remote_copy(
+            src_ref=pot_ref.at[plane, pl.ds(pl.multiple_of(8 * tile, 8), 8)],
+            dst_ref=pot_piece(source, quarter),
+            send_sem=pot_send.at[k], recv_sem=pot_recv.at[source],
+            device_id=(lax.rem(me + k, 24), band), device_id_type=MESH,
+        )
+
+    def in_copy(k, source):
+        peer = lax.rem(me + k, 24)
+        return pltpu.make_async_remote_copy(
+            src_ref=orbs_ref.at[peer], dst_ref=field.at[pl.ds(2 + 2 * source, 2)],
+            send_sem=in_send.at[k], recv_sem=in_recv.at[source],
+            device_id=(peer, band), device_id_type=MESH,
+        )
+
+    def start_pot(k, carry):
+        pot_copy(k, me).start()
+        return carry
+
+    lax.fori_loop(1, 24, start_pot, 0)
+
+    def start_in(k, carry):
+        in_copy(k, me).start()
+        return carry
+
+    lax.fori_loop(1, 24, start_in, 0)
+    field[pl.ds(2 + 2 * me, 2)] = orbs_ref[me]
+    pot[2 * me + plane, pl.ds(pl.multiple_of(8 * tile, 8), 8)] = pot_ref[
+        plane, pl.ds(pl.multiple_of(8 * tile, 8), 8)
+    ]
+
+    def wait_pot(k, carry):
+        pot_copy(k, lax.rem(me + k, 24)).wait_recv()
+        return carry
+
+    lax.fori_loop(1, 24, wait_pot, 0)
+
+    def share(k, q):
+        place = pot4.at[:, lax.div(q, 2), pl.ds(pl.multiple_of(8 * lax.rem(q, 2), 8), 8)]
+        return pltpu.make_async_remote_copy(
+            src_ref=place, dst_ref=place,
+            send_sem=share_send.at[k], recv_sem=share_recv.at[q],
+            device_id=friend(k)[1], device_id_type=MESH,
+        )
+
+    pot4 = pot.reshape(24, 2, 16, LANES)
+    for k in range(1, 4):
+        share(k, quarter).start()
+
+    def wait_in(k, carry):
+        in_copy(k, lax.rem(me + k, 24)).wait_recv()
+        return carry
+
+    lax.fori_loop(1, 24, wait_in, 0)
+    for k in range(1, 4):
+        share(k, friend(k)[0]).wait_recv()
+
+    lane = lax.broadcasted_iota(jnp.int32, (4, 16, LANES), 2)
+    even = lane < NZ
+    deep = lax.rem(lane, NZ)
+
+    def applied(source, at):
+        center = source[pl.ds(at + 2, 4)]
+        near = source[pl.ds(at + 1, 4)] + source[pl.ds(at + 3, 4)]
+        far = source[pl.ds(at, 4)] + source[pl.ds(at + 4, 4)]
+        swap = pltpu.roll(center, NZ, axis=2)
+        near = near + swap + jnp.where(even, pltpu.roll(swap, 1, axis=1), pltpu.roll(swap, 15, axis=1))
+        far = far + pltpu.roll(center, 1, axis=1) + pltpu.roll(center, 15, axis=1)
+        near = near + pltpu.roll(jnp.where(deep == 0, swap, center), LANES - 1, axis=2)
+        near = near + pltpu.roll(jnp.where(deep == NZ - 1, swap, center), 1, axis=2)
+        far = far + pltpu.roll(jnp.where(deep < 2, swap, center), LANES - 2, axis=2)
+        far = far + pltpu.roll(jnp.where(deep >= NZ - 2, swap, center), 2, axis=2)
+        level = (pot[pl.ds(at, 4)] - 2.25) * 0.25
+        return level * center - near * (1.0 / 6.0) + far * (1.0 / 96.0)
+
+    def wrapped(target):
+        target[0:2] = target[48:50]
+        target[50:52] = target[2:4]
+
+    wrapped(field)
+
+    def stage_1(i, carry):
+        first[pl.ds(4 * i + 2, 4)] = applied(field, 4 * i)
+        return carry
+
+    lax.fori_loop(0, 12, stage_1, 0)
+    wrapped(first)
+
+    def stage_2(i, carry):
+        second[pl.ds(4 * i + 2, 4)] = 2.0 * applied(first, 4 * i) - field[pl.ds(4 * i + 2, 4)]
+        return carry
+
+    lax.fori_loop(0, 12, stage_2, 0)
+    wrapped(second)
+
+    def stage_3(i, carry):
+        last[pl.ds(4 * i, 4)] = 2.0 * applied(second, 4 * i) - first[pl.ds(4 * i + 2, 4)]
+        return carry
+
+    lax.fori_loop(0, 12, stage_3, 0)
+
+    def back_copy(k, orbital):
+        peer = lax.rem(me + k, 24)
+        return pltpu.make_async_remote_copy(
+            src_ref=last.at[pl.ds(2 * peer, 2)], dst_ref=home_ref.at[orbital],
+            send_sem=back_send.at[k], recv_sem=back_recv.at[orbital],
+            device_id=(peer, band), device_id_type=MESH,
+        )
+
+    def start_back(k, carry):
+        back_copy(k, me).start()
+        return carry
+
+    lax.fori_loop(1, 24, start_back, 0)
+    home_ref[me] = last[pl.ds(2 * me, 2)]
+
+    def finish(k, carry):
+        back_copy(k, lax.rem(me + k, 24)).wait_recv()
+        return carry
+
+    lax.fori_loop(1, 24, finish, 0)
+
+    def sent(k, carry):
+        pot_copy(k, me).wait_send()
+        in_copy(k, me).wait_send()
+        back_copy(k, me).wait_send()
+        return carry
+
+    lax.fori_loop(1, 24, sent, 0)
+    for k in range(1, 4):
+        share(k, quarter).wait_send()
+
+
+def filtered_of(orbitals, potential):
+    dma = pltpu.SemaphoreType.DMA
+    padded = pltpu.VMEM((52, 16, LANES), jnp.float32)
+    vmem = pl.BlockSpec(memory_space=pltpu.VMEM)
+    return pl.pallas_call(
+        filter_kernel,
+        out_shape=jax.ShapeDtypeStruct((ROWS, 2, 16, LANES), jnp.float32),
+        in_specs=[vmem, vmem],
+        out_specs=vmem,
+        scratch_shapes=[
+            padded, padded, padded,
+            pltpu.VMEM((48, 16, LANES), jnp.float32), pltpu.VMEM((48, 16, LANES), jnp.float32),
+            dma((24,)), dma((24,)), dma((24,)), dma((24,)), dma((4,)), dma((4,)), dma((24,)), dma((24,)),
+        ],
+        compiler_params=pltpu.CompilerParams(collective_id=1, has_side_effects=True),
+    )(orbitals.reshape(ROWS, 2, 16, LANES), potential.reshape(2, 16, LANES))
 
 
 def shards(orbitals, potential):
-    filtered = chebyshev(orbitals, potential, apply_hamiltonian)
+    filtered = filtered_of(orbitals, potential).reshape(ROWS, 2, 2048)
     return (filtered, margin_of(filtered))
 
 

time: 180 us -> 130 us (0.72); the launches traced: 177 us -> 130 us
  Pallas kernels: 73.2 us -> 122 us
  waiting for transfers between devices: 35.5 us -> 0 us
  starting transfers between devices: 29.2 us -> 0 us
  other arithmetic: 22.9 us -> 0 us
  local copies, waits for them, and re-layouts: 15.7 us -> 7.14 us
    pallas_call x0 -> x1, Pallas kernels: none -> 52.6 us  [filtered_of(): pl.pallas_call(filter_kernel, out_shape=jax.ShapeDtypeStruct((ROWS, 2, 16...]
    ppermute x6 -> x0, waiting for transfers between devices: 35.5 us -> none  [the longest x3 31.8 us: padded_2(): lax.ppermute(tail, axis, [(i, (i + 1) % count) for i in range(count)])]
    ppermute x6 -> x0, starting transfers between devices: 29.2 us -> none  [the longest x3 23.3 us: padded_2(): lax.ppermute(head, axis, [((i + 1) % count, i) for i in range(count)])]
    sub x2 -> x0, other arithmetic: 15.3 us -> none  [the longest x1 7.67 us: chebyshev(): return 2.0 * (operator(second, potential) - 6.0 * second) / 4.0 - first]
    slice x36 -> x0, local copies, waits for them, and re-layouts: 12.2 us -> none  [the longest x12 4.92 us: shift_plane(): direct = jnp.roll(flat, -step, axis=-1)]
    div x1 -> x0, other arithmetic: 7.53 us -> none  [chebyshev(): first = (operator(block, potential) - 6.0 * block) / 4.0]
    pallas_call x1, Pallas kernels: 73.2 us -> 69.8 us  [margin_of(): pl.pallas_call(margin_kernel, out_shape=jax.ShapeDtypeStruct((ROWS, TILES...]
    pallas_call x0 -> x1, local copies, waits for them, and re-layouts: none -> 1.97 us  [filtered_of(): pl.pallas_call(filter_kernel, out_shape=jax.ShapeDtypeStruct((ROWS, 2, 16...]
  transfers between devices with their start and end apart: 6 -> 0, of which waited for: 5 -> 0; matrix products, arithmetic and copies ran while one was open for 6% -> 0% of each run, Pallas kernels for 0% -> 0%
where the time goes in v2:
time: 130 us
  Pallas kernels  122 us (94%)
  local copies, waits for them, and re-layouts  7.14 us (5%)
    pallas_call x1, Pallas kernels, margin_of(): pl.pallas_call(margin_kernel, out_shape=jax.ShapeDtypeStruct((ROWS, TILES...  69.8 us
    pallas_call x1, Pallas kernels, filtered_of(): pl.pallas_call(filter_kernel, out_shape=jax.ShapeDtypeStruct((ROWS, 2, 16...  52.6 us

profile of v2, /device:TPU:1, one launch (start us, length us, event | category | flops | bytes accessed | tf_op | source)
XLA Modules:
  0.0 130.2 jit_solution(1881797167751320090)
XLA Ops:
  0.6 0.0 copy-start.1
  0.6 2.1 %reshape.16.orbs_ref = f32[24,2,16,128]{3,2,1,0:T(8,128)} reshape(f32[24,2,2048]{2,1,0:T(2,128)} %param.2) | data formatting | bytes 786432 | tf_op jit(solution)/shard_map/reshape | solution.py:467
  2.7 0.0 copy-done.1
  2.7 0.6 copy.11
  3.3 52.6 %shard_map.41 = f32[24,2,16,128]{3,2,1,0:T(8,128)} custom-call(f32[24,2,16,128]{3,2,1,0:T(8,128)} %reshape.16.orbs_ref, f32[2,16,128]{2,1,0:T(8,128)} %bitcast.16), custom_call_target="tpu_custom_call" | custom-call | tf_op jit(solution)/shard_map/pallas_call | solution.py:456
  55.9 2.0 %copy.5 = f32[24,2,16,128]{3,0,2,1:T(8,128)} copy(f32[24,2,16,128]{3,2,1,0:T(8,128)} %shard_map.41) | data formatting | bytes 786432 | tf_op jit(solution)/shard_map/pallas_call | solution.py:456
  57.9 0.0 copy-start
  57.9 69.8 %shard_map.42 = f32[24,6,128]{2,1,0:T(8,128)} custom-call(f32[32,24,128]{2,1,0:T(8,128)} %bitcast.13), custom_call_target="tpu_custom_call" | custom-call | tf_op jit(solution)/shard_map/pallas_call | solution.py:265
  127.7 1.5 %copy.10 = f32[3,8,6,128]{3,1,2,0:T(8,128)} copy(f32[3,8,6,128]{3,2,1,0:T(8,128)} %bitcast.14) | data formatting | bytes 147456
  129.3 0.0 copy-done
  129.3 0.9 reshape.18
Async XLA Ops:
  0.6 2.1 %copy-start.1 = (f32[2,2048]{1,0:T(2,128)S(1)}, f32[2,2048]{1,0:T(2,128)}, u32[]{:S(2)}) copy-start(f32[2,2048]{1,0:T(2,128)} %param.3) | copy-start | bytes 49156
  57.9 71.4 %copy-start = (f32[24,2,16,128]{3,2,1,0:T(8,128)S(1)}, f32[24,2,16,128]{3,2,1,0:T(8,128)}, u32[]{:S(2)}) copy-start(f32[24,2,16,128]{3,2,1,0:T(8,128)} %shard_map.41) | copy-start | bytes 1179652

commit v3 on v0

v3 whole, which is shorter than its diff:
```python
import jax
import jax.numpy as jnp
from jax import lax
from jax.experimental import pallas as pl
from jax.experimental.pallas import tpu as pltpu
from jax.sharding import PartitionSpec as P

MESH = pl.DeviceIdType.MESH
NZ_LO, N_Y = 6, 8
SPACE = 24
SPOTS = 2 * SPACE
NZ = 64
ROWS = 24
ORBS = 768
LANES = 128
TILES = ORBS // LANES
CELLS = 48 * 2048


def kernel(
    orbs_ref, pot_ref, home_ref, margin_ref,
    field, first, second, last, pot, column, held, rows, cat, part, ring, mine, pieces, done,
    in_send, in_recv, pot_send, pot_recv, share_send, share_recv, col_send, col_recv,
    meet_send, meet_recv, core_send, core_recv, home_send, home_recv,
    ring_send, ring_recv, piece_send, piece_recv, out_send, out_recv,
):
    me, band = lax.axis_index("space"), lax.axis_index("band")
    core, pair = lax.rem(band, 2), lax.div(band, 2)
    y, z_hi = lax.rem(pair, N_Y), lax.div(pair, N_Y)
    spot = z_hi * SPACE + me
    seat = 2 * y + core

    def band_of(hi, a_y):
        return (hi * N_Y + a_y) * 2 + core

    def spot_device(index):
        return (lax.rem(index, SPACE), band_of(lax.div(index, SPACE), y))

    def seat_device(index):
        return (me, z_hi * 2 * N_Y + index)

    other = seat_device(2 * y + 1 - core)
    up = (me, band_of(z_hi, lax.rem(y + 1, N_Y)))
    down = (me, band_of(z_hi, lax.rem(y + N_Y - 1, N_Y)))

    def copy(source, target, send, recv, peer):
        return pltpu.make_async_remote_copy(
            src_ref=source, dst_ref=target, send_sem=send, recv_sem=recv,
            device_id=peer, device_id_type=MESH,
        )

    def each(low, high, body):
        def step(k, carry):
            body(k)
            return carry

        lax.fori_loop(low, high, step, 0)

    barrier = pltpu.get_barrier_semaphore()

    def greet(peer):
        pl.semaphore_signal(barrier, inc=1, device_id=peer, device_id_type=MESH)

    each(1, SPOTS, lambda k: greet(spot_device(lax.rem(spot + k, SPOTS))))
    each(1, 2 * N_Y, lambda k: greet(seat_device(lax.rem(seat + k, 2 * N_Y))))
    pl.semaphore_wait(barrier, SPOTS - 1 + 2 * N_Y - 1)

    def pot_copy(k, source):
        peer = lax.rem(me + k, SPACE)
        return copy(
            pot_ref.at[pl.ds(2 * seat, 2)], pot.at[source, pl.ds(2 * seat, 2)],
            pot_send.at[k], pot_recv.at[source], (peer, band),
        )

    def in_copy(k, source):
        peer = lax.rem(me + k, SPACE)
        return copy(
            orbs_ref.at[peer], field.at[1 + source],
            in_send.at[k], in_recv.at[source], (peer, band),
        )

    each(1, SPACE, lambda k: pot_copy(k, me).start())
    each(1, SPACE, lambda k: in_copy(k, me).start())
    field[1 + me] = orbs_ref[me]
    own_pot = pltpu.make_async_copy(
        pot_ref.at[pl.ds(2 * seat, 2)], pot.at[me, pl.ds(2 * seat, 2)], pot_recv.at[me]
    )
    own_pot.start()
    each(1, SPACE, lambda k: pot_copy(k, lax.rem(me + k, SPACE)).wait_recv())
    own_pot.wait()

    def share(k, source):
        place = pot.at[:, pl.ds(2 * source, 2)]
        return copy(
            place, place, share_send.at[k], share_recv.at[source],
            seat_device(lax.rem(seat + k, 2 * N_Y)),
        )

    each(1, 2 * N_Y, lambda k: share(k, seat).start())
    each(1, SPACE, lambda k: in_copy(k, lax.rem(me + k, SPACE)).wait_recv())
    each(1, 2 * N_Y, lambda k: share(k, lax.rem(seat + k, 2 * N_Y)).wait_recv())

    lane = lax.broadcasted_iota(jnp.int32, (2, 32, LANES), 2)
    row = lax.broadcasted_iota(jnp.int32, (2, 32, LANES), 1)
    low_half = lane < NZ
    deep = lax.rem(lane, NZ)
    low_plane = lax.rem(row, 2) == 0

    def applied(source, at):
        center = source[pl.ds(at + 1, 2)]
        before = source[pl.ds(at, 2)]
        after = source[pl.ds(at + 2, 2)]
        swap = pltpu.roll(center, NZ, axis=2)
        near = jnp.where(
            low_plane,
            pltpu.roll(center + before, 31, axis=1),
            pltpu.roll(center + after, 1, axis=1),
        )
        far = before + after
        near = near + swap + jnp.where(
            low_half, pltpu.roll(swap, 2, axis=1), pltpu.roll(swap, 30, axis=1)
        )
        far = far + pltpu.roll(center, 2, axis=1) + pltpu.roll(center, 30, axis=1)
        near = near + pltpu.roll(jnp.where(deep == 0, swap, center), LANES - 1, axis=2)
        near = near + pltpu.roll(jnp.where(deep == NZ - 1, swap, center), 1, axis=2)
        far = far + pltpu.roll(jnp.where(deep < 2, swap, center), LANES - 2, axis=2)
        far = far + pltpu.roll(jnp.where(deep >= NZ - 2, swap, center), 2, axis=2)
        level = (pot[pl.ds(at, 2)] - 2.25) * 0.25
        return level * center - near * (1.0 / 6.0) + far * (1.0 / 96.0)

    def wrapped(target):
        target[0] = target[SPACE]
        target[SPACE + 1] = target[1]

    def stage_1(i):
        first[pl.ds(2 * i + 1, 2)] = applied(field, 2 * i)

    def stage_2(i):
        second[pl.ds(2 * i + 1, 2)] = 2.0 * applied(first, 2 * i) - field[pl.ds(2 * i + 1, 2)]

    def stage_3(i):
        last[pl.ds(2 * i, 2)] = 2.0 * applied(second, 2 * i) - first[pl.ds(2 * i + 1, 2)]

    wrapped(field)
    each(0, 12, stage_1)
    wrapped(first)
    each(0, 12, stage_2)
    wrapped(second)
    each(0, 12, stage_3)

    def col_copy(tile, k, source):
        peer = lax.rem(spot + k, SPOTS)
        return copy(
            last.at[
                lax.rem(peer, SPACE),
                pl.ds(pl.multiple_of(16 * lax.div(peer, SPACE) + 8 * tile, 8), 8),
            ],
            column.at[lax.div(source, SPACE), lax.rem(source, SPACE), pl.ds(8 * tile, 8)],
            col_send.at[tile, k], col_recv.at[tile, source], spot_device(peer),
        )

    for tile in range(2):
        each(1, SPOTS, lambda k: col_copy(tile, k, spot).start())
    column[z_hi, me] = last[me, pl.ds(pl.multiple_of(16 * z_hi, 8), 16)]
    home_ref[me] = last[me]

    def band_place(k, hi, a_y):
        return held.at[k, pl.ds(pl.multiple_of(ROWS * band_of(hi, a_y), 8), ROWS)]

    def meet_copy(k, hi, a_y, source):
        return copy(
            column.at[hi, :, 8 * lax.rem(a_y, 2) + 2 * lax.div(a_y, 2) + k],
            band_place(k, hi, source),
            meet_send.at[hi, k, a_y], meet_recv.at[hi, k, source],
            (me, band_of(z_hi, a_y)),
        )

    def own_copy(k, hi):
        return pltpu.make_async_copy(
            column.at[hi, :, 8 * lax.rem(y, 2) + 2 * lax.div(y, 2) + k],
            band_place(k, hi, y), meet_recv.at[hi, k, y],
        )

    for tile in range(2):
        each(1, SPOTS, lambda k: col_copy(tile, k, lax.rem(spot + k, SPOTS)).wait_recv())

        def meet(i):
            a_y = 2 * lax.rem(lax.div(y, 2) + i, 4) + tile

            @pl.when(a_y != y)
            def _():
                for hi in range(2):
                    for k in range(2):
                        meet_copy(k, hi, a_y, y).start()

            @pl.when(a_y == y)
            def _():
                for hi in range(2):
                    for k in range(2):
                        own_copy(k, hi).start()

        each(0, 4, meet)

    def home_copy(k, orbital):
        peer = lax.rem(me + k, SPACE)
        return copy(
            last.at[peer], home_ref.at[orbital],
            home_send.at[k], home_recv.at[orbital], (peer, band),
        )

    each(1, SPACE, lambda k: home_copy(k, me).start())

    def across(j, a_core):
        place = held.at[:, pl.ds(pl.multiple_of(ROWS * (2 * j + a_core), 8), ROWS)]
        return copy(place, place, core_send.at[j], core_recv.at[j], other)

    for hi in range(2):
        for k in range(2):
            own_copy(k, hi).wait()
        across(hi * N_Y + y, core).start()

    def arrived(i):
        source = lax.rem(y + i, N_Y)
        for hi in range(2):
            for k in range(2):
                meet_copy(k, hi, source, source).wait_recv()
            across(hi * N_Y + source, core).start()

    each(1, N_Y, arrived)
    each(0, 2 * N_Y, lambda j: across(j, 1 - core).wait_recv())

    for g in range(2 * N_Y):
        for k in range(2):
            rows[g, :, LANES * k:LANES * (k + 1)] = held[
                k, pl.ds(pl.multiple_of(ROWS * (2 * g + core), 8), ROWS), :
            ]
    left = rows[...].reshape(2 * N_Y * ROWS, 2 * LANES)
    left_hi = left.astype(jnp.bfloat16)
    left_lo = (left - left_hi.astype(jnp.float32)).astype(jnp.bfloat16)
    left_cat = jnp.concatenate([left_hi, left_hi, left_lo], axis=1)
    for k in range(2):
        cells = held[k]
        cells_hi = cells.astype(jnp.bfloat16)
        cells_lo = (cells - cells_hi.astype(jnp.float32)).astype(jnp.bfloat16)
        for slot, value in enumerate((cells_hi, cells_lo, cells_hi)):
            cat[:, 2 * LANES * slot + LANES * k:2 * LANES * slot + LANES * (k + 1)] = value
    for n in range(3):
        block = lax.dot_general(
            left_cat, cat[256 * n:256 * (n + 1), :], (((1,), (1,)), ((), ())),
            preferred_element_type=jnp.float32,
        )
        part[:, :, :, 256 * n:256 * (n + 1)] = block.reshape(2, N_Y, ROWS, 256)

    def hop(way, step, h, source):
        return copy(
            source, ring.at[way, step, h],
            ring_send.at[way, step, h], ring_recv.at[way, step, h], up if way == 0 else down,
        )

    def goal(way, step):
        return lax.rem(y + (4 - step if way == 0 else N_Y - 4 + step), N_Y)

    for way in range(2):
        hop(way, 0, way, part.at[way, goal(way, 0)]).start()
    for way in range(2):
        hop(way, 1, 1 - way, part.at[1 - way, goal(way, 1)]).start()
    for step in range(4):
        for turn in range(2 if step else 1):
            for way in range(2):
                h = way if turn == 1 or step == 0 else 1 - way
                slot = ring.at[way, step, h]
                hop(way, step, h, slot).wait_recv()
                if step < 3:
                    ring[way, step, h] = ring[way, step, h] + part[h, goal(way, step + 1)]
                    hop(way, step + 1, h, slot).start()

    for h in range(2):
        total = part[h, y] + ring[0, 3, h] + ring[1, 3, h]
        for t in range(TILES):
            mine[ROWS * h:ROWS * (h + 1), t, :] = total[:, LANES * t:LANES * (t + 1)]

    def piece(k, source):
        peer = lax.rem(spot + k, SPOTS)
        return copy(
            mine.at[peer], pieces.at[source],
            piece_send.at[k], piece_recv.at[source], spot_device(peer),
        )

    each(1, SPOTS, lambda k: piece(k, spot).start())
    pieces[spot] = mine[spot]
    each(1, SPOTS, lambda k: piece(k, lax.rem(spot + k, SPOTS)).wait_recv())
    done[me] = jnp.sum(pieces[...], axis=0) * (1.0 / CELLS)

    def give(k, source):
        peer = lax.rem(me + k, SPACE)
        return copy(
            done.at[me], done.at[source], out_send.at[k], out_recv.at[source], (peer, band)
        )

    each(1, SPACE, lambda k: give(k, me).start())
    each(1, SPACE, lambda k: give(k, lax.rem(me + k, SPACE)).wait_recv())
    for t in range(TILES):
        margin_ref[:, LANES * t:LANES * (t + 1)] = done[:, t, :]

    def finish(k):
        home_copy(k, lax.rem(me + k, SPACE)).wait_recv()
        for sent in (pot_copy, in_copy, home_copy, give):
            sent(k, me).wait_send()

    each(1, SPACE, finish)
    each(1, 2 * N_Y, lambda k: share(k, seat).wait_send())

    def finish_spots(k):
        for tile in range(2):
            col_copy(tile, k, spot).wait_send()
        piece(k, spot).wait_send()

    each(1, SPOTS, finish_spots)

    def finish_meet(i):
        for hi in range(2):
            for k in range(2):
                meet_copy(k, hi, lax.rem(y + i, N_Y), y).wait_send()

    each(1, N_Y, finish_meet)
    each(0, 2 * N_Y, lambda j: across(j, core).wait_send())
    for way in range(2):
        for step in range(4):
            for h in range(2):
                if step > 0 or h == way:
                    hop(way, step, h, ring.at[way, step, h]).wait_send()


def shards(orbitals, potential):
    dma = pltpu.SemaphoreType.DMA
    f32 = jnp.float32
    vmem = pl.BlockSpec(memory_space=pltpu.VMEM)
    padded = pltpu.VMEM((SPACE + 2, 32, LANES), f32)
    home, margin = pl.pallas_call(
        kernel,
        out_shape=(
            jax.ShapeDtypeStruct((ROWS, 32, LANES), f32),
            jax.ShapeDtypeStruct((ROWS, ORBS), f32),
        ),
        in_specs=[vmem, vmem],
        out_specs=(vmem, vmem),
        scratch_shapes=[
            padded, padded, padded,
            pltpu.VMEM((SPACE, 32, LANES), f32),
            pltpu.VMEM((SPACE, 32, LANES), f32),
            pltpu.VMEM((2, SPACE, 16, LANES), f32),
            pltpu.VMEM((2, ORBS, LANES), f32),
            pltpu.VMEM((2 * N_Y, ROWS, 2 * LANES), f32),
            pltpu.VMEM((ORBS, 6 * LANES), jnp.bfloat16),
            pltpu.VMEM((2, N_Y, ROWS, ORBS), f32),
            pltpu.VMEM((2, 4, 2, ROWS, ORBS), f32),
            pltpu.VMEM((SPOTS, TILES, LANES), f32),
            pltpu.VMEM((SPOTS, TILES, LANES), f32),
            pltpu.VMEM((ROWS, TILES, LANES), f32),
            dma((SPACE,)), dma((SPACE,)), dma((SPACE,)), dma((SPACE,)),
            dma((2 * N_Y,)), dma((2 * N_Y,)), dma((2, SPOTS)), dma((2, SPOTS)),
            dma((2, 2, N_Y)), dma((2, 2, N_Y)), dma((2 * N_Y,)), dma((2 * N_Y,)),
            dma((SPACE,)), dma((SPACE,)),
            dma((2, 4, 2)), dma((2, 4, 2)), dma((SPOTS,)), dma((SPOTS,)), dma((SPACE,)), dma((SPACE,)),
        ],
        compiler_params=pltpu.CompilerParams(collective_id=0, has_side_effects=True),
    )(
        orbitals.reshape(ROWS, 2, 16, LANES).transpose(0, 2, 1, 3).reshape(ROWS, 32, LANES),
        potential.reshape(2, 16, LANES).transpose(1, 0, 2).reshape(32, LANES),
    )
    filtered = home.reshape(ROWS, 16, 2, LANES).transpose(0, 2, 1, 3).reshape(ROWS, 2, 2048)
    return (filtered, margin)


def solution(mesh):
    return jax.shard_map(
        shards,
        mesh=mesh,
        in_specs=(P("band", "space", None), P("space", None)),
        out_specs=(P("band", "space", None), P("band", None)),
        check_vma=False,
    )
```

time: 372 us -> 114 us (0.31)
  waiting for transfers between devices: 179 us -> 0 us
  Pallas kernels: 0 us -> 109 us
  blocking collectives: 103 us -> 0 us
  starting transfers between devices: 29.3 us -> 0 us
  other arithmetic: 23.6 us -> 0 us
  local copies, waits for them, and re-layouts: 16.2 us -> 2.44 us
  between operations: 14.3 us -> 0.65 us
    reduce_scatter x1 -> x0, waiting for transfers between devices: 146 us -> none  [shards(): lax.psum_scatter(partial_sum, 'band', scatter_dimension=0, tiled=True)]
    pallas_call x0 -> x1, Pallas kernels: none -> 109 us  [shards(): pl.pallas_call(kernel, out_shape=(jax.ShapeDtypeStruct((ROWS, 32, LANES),...]
    all_to_all x2 -> x0, blocking collectives: 103 us -> none  [the longest x1 63.7 us: from_everyone(): lax.all_to_all(jnp.broadcast_to(shard[None], (size, *shard.shape)), axis,...]
    ppermute x6 -> x0, waiting for transfers between devices: 33.2 us -> none  [the longest x3 29.5 us: padded_2(): lax.ppermute(tail, axis, [(i, (i + 1) % count) for i in range(count)])]
    ppermute x6 -> x0, starting transfers between devices: 29.2 us -> none  [the longest x3 23.3 us: padded_2(): lax.ppermute(head, axis, [((i + 1) % count, i) for i in range(count)])]
    sub x2 -> x0, other arithmetic: 15.3 us -> none  [the longest x1 7.67 us: chebyshev(): return 2.0 * (operator(second, potential) - 6.0 * second) / 4.0 - first]
    slice x36 -> x0, local copies, waits for them, and re-layouts: 14.7 us -> none  [the longest x12 4.92 us: shift_plane(): direct = jnp.roll(flat, -step, axis=-1)]
    div x1 -> x0, other arithmetic: 7.52 us -> none  [chebyshev(): first = (operator(block, potential) - 6.0 * block) / 4.0]
  transfers between devices with their start and end apart: 7 -> 0, of which waited for: 6 -> 0; matrix products, arithmetic and copies ran while one was open for 4% -> 0% of each run, Pallas kernels for 0% -> 0%
where the time goes in v3:
time: 114 us; the launch traced here: 113 us
  Pallas kernels  109 us (96%)
  local copies, waits for them, and re-layouts  2.44 us (2%)
    pallas_call x1, Pallas kernels, shards(): pl.pallas_call(kernel, out_shape=(jax.ShapeDtypeStruct((ROWS, 32, LANES),...  109 us
    unnamed x4, local copies, waits for them, and re-layouts  2.44 us

profile of v3, /device:TPU:1, one launch (start us, length us, event | category | flops | bytes accessed | tf_op | source)
XLA Modules:
  0.0 112.5 jit_solution(6074127774887920746)
XLA Ops:
  0.6 109.5 %shard_map.41 = (f32[24,32,128]{2,1,0:T(8,128)}, f32[24,768]{1,0:T(8,128)}) custom-call(f32[24,32,128]{2,1,0:T(8,128)} %bitcast.15, f32[32,128]{1,0:T(8,128)} %bitcast.17), custom_call_target="tpu_custom_call" | custom-call | tf_op jit(solution)/shard_map/pallas_call | solution.py:339
  110.1 0.0 copy-start
  110.1 1.8 %copy.9 = f32[24,2,2048]{2,1,0:T(2,128)} copy(f32[24,2,2048]{2,1,0:T(2,128)} %bitcast.16) | data formatting | bytes 786432
  111.9 0.0 copy-done
  111.9 0.6 copy.10
Async XLA Ops:
  110.1 1.8 %copy-start = (f32[24,768]{1,0:T(8,128)S(1)}, f32[24,768]{1,0:T(8,128)}, u32[]{:S(2)}) copy-start(f32[24,768]{1,0:T(8,128)} %get-tuple-element.9) | copy-start | bytes 221188

commit v4 on v3

v4 whole, which is shorter than its diff:
```python
import jax
import jax.numpy as jnp
from jax import lax
from jax.experimental import pallas as pl
from jax.experimental.pallas import tpu as pltpu
from jax.sharding import PartitionSpec as P

MESH = pl.DeviceIdType.MESH
NZ_LO, N_Y = 6, 8
SPACE = 24
SPOTS = 2 * SPACE
NZ = 64
ROWS = 24
ORBS = 768
LANES = 128
TILES = ORBS // LANES
CELLS = 48 * 2048
EARLY = 24


def kernel(
    orbs_ref, pot_ref, home_ref, margin_ref,
    field, first, second, last, pot, column, held, rows, cat, part, ring, mine, pieces, done,
    in_send, in_recv, pot_send, pot_recv, share_send, share_recv, col_send, col_recv,
    meet_send, meet_recv, core_send, core_recv, home_send, home_recv,
    ring_send, ring_recv, piece_send, piece_recv, out_send, out_recv, near_sem,
):
    me, band = lax.axis_index("space"), lax.axis_index("band")
    core, pair = lax.rem(band, 2), lax.div(band, 2)
    y, z_hi = lax.rem(pair, N_Y), lax.div(pair, N_Y)
    spot = z_hi * SPACE + me
    seat = 2 * y + core

    def wrap(value, size):
        return jnp.where(value >= size, value - size, value)

    def split(index):
        hi = jnp.where(index >= SPACE, 1, 0)
        return hi, index - SPACE * hi

    def arrival(target, semaphore):
        pltpu.make_async_copy(target, target, semaphore).wait()

    def band_of(hi, a_y):
        return (hi * N_Y + a_y) * 2 + core

    def spot_device(index):
        hi, rest = split(index)
        return (rest, band_of(hi, y))

    def seat_device(index):
        return (me, z_hi * 2 * N_Y + index)

    other = seat_device(2 * y + 1 - core)
    up = (me, band_of(z_hi, wrap(y + 1, N_Y)))
    down = (me, band_of(z_hi, wrap(y + N_Y - 1, N_Y)))

    def copy(source, target, send, recv, peer):
        return pltpu.make_async_remote_copy(
            src_ref=source, dst_ref=target, send_sem=send, recv_sem=recv,
            device_id=peer, device_id_type=MESH,
        )

    def each(low, high, body):
        def step(k, carry):
            body(k)
            return carry

        lax.fori_loop(low, high, step, 0)

    closers = []
    barrier = pltpu.get_barrier_semaphore()

    def greet(peer):
        pl.semaphore_signal(barrier, inc=1, device_id=peer, device_id_type=MESH)

    each(1, SPOTS, lambda k: greet(spot_device(wrap(spot + k, SPOTS))))
    each(1, 2 * N_Y, lambda k: greet(seat_device(wrap(seat + k, 2 * N_Y))))
    pl.semaphore_wait(barrier, SPOTS - 1 + 2 * N_Y - 1)

    def pot_copy(k, source):
        peer = wrap(me + k, SPACE)
        return copy(
            pot_ref.at[pl.ds(2 * seat, 2)], pot.at[source, pl.ds(2 * seat, 2)],
            pot_send.at[k], pot_recv.at[source], (peer, band),
        )

    def in_copy(k, source):
        peer = wrap(me + k, SPACE)
        return copy(
            orbs_ref.at[peer], field.at[1 + source],
            in_send.at[k], in_recv.at[source], (peer, band),
        )

    each(1, SPACE, lambda k: pot_copy(k, me).start())
    each(1, SPACE, lambda k: in_copy(k, me).start())
    closers.append(lambda: each(1, SPACE, lambda k: pot_copy(k, me).wait_send()))
    closers.append(lambda: each(1, SPACE, lambda k: in_copy(k, me).wait_send()))
    pltpu.make_async_copy(orbs_ref.at[me], field.at[1 + me], in_recv.at[me]).start()
    pltpu.make_async_copy(
        pot_ref.at[pl.ds(2 * seat, 2)], pot.at[me, pl.ds(2 * seat, 2)], pot_recv.at[me]
    ).start()
    each(0, SPACE, lambda j: arrival(pot.at[j, pl.ds(2 * seat, 2)], pot_recv.at[j]))

    def share(k, source):
        place = pot.at[:, pl.ds(2 * source, 2)]
        return copy(
            place, place, share_send.at[k], share_recv.at[source],
            seat_device(wrap(seat + k, 2 * N_Y)),
        )

    each(1, 2 * N_Y, lambda k: share(k, seat).start())
    closers.append(lambda: each(1, 2 * N_Y, lambda k: share(k, seat).wait_send()))
    each(0, SPACE, lambda j: arrival(field.at[1 + j], in_recv.at[j]))
    each(1, 2 * N_Y, lambda k: share(k, wrap(seat + k, 2 * N_Y)).wait_recv())

    shape = (2, 32, LANES)
    lane = lax.broadcasted_iota(jnp.int32, shape, 2)
    low_half = lane < NZ
    deep = lane & (NZ - 1)
    low_plane = (lax.broadcasted_iota(jnp.int32, shape, 1) & 1) == 0
    near_weight, far_weight = -1.0 / 6.0, 1.0 / 96.0

    def applied(source, at):
        center = source[pl.ds(at + 1, 2)]
        before = source[pl.ds(at, 2)]
        after = source[pl.ds(at + 2, 2)]
        swap = pltpu.roll(center, NZ, axis=2)
        pairs = (center + jnp.where(low_plane, after, before)).reshape(8, 8, LANES)
        near = jnp.where(
            low_plane,
            pltpu.roll(pairs, 7, axis=1).reshape(shape),
            pltpu.roll(pairs, 1, axis=1).reshape(shape),
        ) + swap
        near = near + pltpu.roll(jnp.where(deep == 0, swap, center), LANES - 1, axis=2)
        near = near + pltpu.roll(jnp.where(deep == NZ - 1, swap, center), 1, axis=2)
        far = before + after
        far = far + pltpu.roll(jnp.where(deep < 2, swap, center), LANES - 2, axis=2)
        far = far + pltpu.roll(jnp.where(deep >= NZ - 2, swap, center), 2, axis=2)
        beside = near_weight * swap
        both = far_weight * center
        shifted = pltpu.roll(jnp.where(low_half, beside + both, both), 2, axis=1)
        shifted = shifted + pltpu.roll(jnp.where(low_half, both, beside + both), 30, axis=1)
        level = (pot[pl.ds(at, 2)] - 2.25) * 0.25
        return level * center + near * near_weight + far * far_weight + shifted

    def wrapped(target):
        target[0] = target[SPACE]
        target[SPACE + 1] = target[1]

    def stage_1(i):
        first[pl.ds(2 * i + 1, 2)] = applied(field, 2 * i)

    def stage_2(i):
        second[pl.ds(2 * i + 1, 2)] = 2.0 * applied(first, 2 * i) - field[pl.ds(2 * i + 1, 2)]

    def col_copy(tile, hi, rest):
        return copy(
            last.at[rest, pl.ds(16 * hi + 8 * tile, 8)],
            column.at[spot, pl.ds(8 * tile, 8)],
            col_send.at[tile, SPACE * hi + rest], col_recv.at[tile, spot], (rest, band_of(hi, y)),
        )

    def start_col(tile, rest):
        for hi in range(2):
            @pl.when((rest != me) | (hi != z_hi))
            def _():
                col_copy(tile, hi, rest).start()

    def stage_3(i):
        j = wrap(begin + i, 12)
        last[pl.ds(2 * j, 2)] = 2.0 * applied(second, 2 * j) - first[pl.ds(2 * j + 1, 2)]
        for n in range(2):
            start_col(0, 2 * j + n)

    wrapped(field)
    each(0, 12, stage_1)
    wrapped(first)
    each(0, 12, stage_2)
    wrapped(second)
    begin = lax.div(me, 2)
    each(0, 12, stage_3)
    each(0, SPACE, lambda k: start_col(1, wrap(me + k, SPACE)))
    for tile in range(2):
        pltpu.make_async_copy(
            last.at[me, pl.ds(pl.multiple_of(16 * z_hi + 8 * tile, 8), 8)],
            column.at[spot, pl.ds(8 * tile, 8)], col_recv.at[tile, spot],
        ).start()

    def finish_col(rest):
        for tile in range(2):
            for hi in range(2):
                @pl.when((rest != me) | (hi != z_hi))
                def _():
                    col_copy(tile, hi, rest).wait_send()

    closers.append(lambda: each(0, SPACE, finish_col))

    def band_place(k, hi, a_y):
        return held.at[k, pl.ds(pl.multiple_of(ROWS * band_of(hi, a_y), 8), ROWS)]

    def meet_copy(k, hi, a_y, source):
        return copy(
            column.at[pl.ds(SPACE * hi, SPACE), 8 * (a_y & 1) + (a_y - (a_y & 1)) + k],
            band_place(k, hi, source),
            meet_send.at[hi, k, a_y], meet_recv.at[hi, k, source],
            (me, band_of(z_hi, a_y)),
        )

    def own_copy(k, hi):
        return pltpu.make_async_copy(
            column.at[pl.ds(SPACE * hi, SPACE), 8 * (y & 1) + (y - (y & 1)) + k],
            band_place(k, hi, y), meet_recv.at[hi, k, y],
        )

    for tile in range(2):
        each(0, SPOTS, lambda j: arrival(column.at[j, pl.ds(8 * tile, 8)], col_recv.at[tile, j]))

        def meet(i):
            a_y = ((y - (y & 1) + 2 * i) & 7) + tile

            @pl.when(a_y != y)
            def _():
                for hi in range(2):
                    for k in range(2):
                        meet_copy(k, hi, a_y, y).start()

            @pl.when(a_y == y)
            def _():
                for hi in range(2):
                    for k in range(2):
                        own_copy(k, hi).start()

        each(0, 4, meet)

    def finish_meet(i):
        for hi in range(2):
            for k in range(2):
                meet_copy(k, hi, (y + i) & 7, y).wait_send()

    closers.append(lambda: each(1, N_Y, finish_meet))

    def across(j, a_core):
        place = held.at[:, pl.ds(pl.multiple_of(ROWS * (2 * j + a_core), 8), ROWS)]
        return copy(place, place, core_send.at[j], core_recv.at[j], other)

    for hi in range(2):
        for k in range(2):
            own_copy(k, hi).wait()
        across(hi * N_Y + y, core).start()

    def arrived(i):
        source = (y + i) & 7
        for hi in range(2):
            for k in range(2):
                meet_copy(k, hi, source, source).wait_recv()
            across(hi * N_Y + source, core).start()

    each(1, N_Y, arrived)
    each(0, 2 * N_Y, lambda j: across(j, 1 - core).wait_recv())
    closers.append(lambda: each(0, 2 * N_Y, lambda j: across(j, core).wait_send()))

    near_rows = pl.multiple_of(16 * z_hi, 8)
    away = pl.multiple_of(16 - 16 * z_hi, 8)

    def home_copy(k, orbital):
        peer = wrap(me + k, SPACE)
        return copy(
            last.at[peer, pl.ds(away, 16)], home_ref.at[orbital, pl.ds(away, 16)],
            home_send.at[k], home_recv.at[orbital], (peer, band),
        )

    each(1, EARLY, lambda k: home_copy(k, me).start())
    near_copy = pltpu.make_async_copy(
        column.at[pl.ds(SPACE * z_hi, SPACE)], home_ref.at[:, pl.ds(near_rows, 16)], near_sem
    )
    near_copy.start()
    closers.append(near_copy.wait)
    pltpu.make_async_copy(
        last.at[me, pl.ds(away, 16)], home_ref.at[me, pl.ds(away, 16)], home_recv.at[me]
    ).start()

    for g in range(2 * N_Y):
        for k in range(2):
            rows[g, :, LANES * k:LANES * (k + 1)] = held[
                k, pl.ds(pl.multiple_of(ROWS * (2 * g + core), 8), ROWS), :
            ]
    left = rows[...].reshape(2 * N_Y * ROWS, 2 * LANES)
    left_hi = left.astype(jnp.bfloat16)
    left_lo = (left - left_hi.astype(jnp.float32)).astype(jnp.bfloat16)
    left_cat = jnp.concatenate([left_hi, left_hi, left_lo], axis=1)
    for k in range(2):
        cells = held[k]
        cells_hi = cells.astype(jnp.bfloat16)
        cells_lo = (cells - cells_hi.astype(jnp.float32)).astype(jnp.bfloat16)
        for slot, value in enumerate((cells_hi, cells_lo, cells_hi)):
            cat[:, 2 * LANES * slot + LANES * k:2 * LANES * slot + LANES * (k + 1)] = value
    for n in range(3):
        block = lax.dot_general(
            left_cat, cat[256 * n:256 * (n + 1), :], (((1,), (1,)), ((), ())),
            preferred_element_type=jnp.float32,
        )
        part[:, :, :, 256 * n:256 * (n + 1)] = block.reshape(2, N_Y, ROWS, 256)

    def hop(way, step, h, source):
        return copy(
            source, ring.at[way, step, h],
            ring_send.at[way, step, h], ring_recv.at[way, step, h], up if way == 0 else down,
        )

    def goal(way, step):
        return (y + (4 - step if way == 0 else 4 + step)) & 7

    for way in range(2):
        hop(way, 0, way, part.at[way, goal(way, 0)]).start()
    for way in range(2):
        hop(way, 1, 1 - way, part.at[1 - way, goal(way, 1)]).start()
    for step in range(4):
        for turn in range(2 if step else 1):
            for way in range(2):
                h = way if turn == 1 or step == 0 else 1 - way
                slot = ring.at[way, step, h]
                hop(way, step, h, slot).wait_recv()
                if step < 3:
                    ring[way, step, h] = ring[way, step, h] + part[h, goal(way, step + 1)]
                    hop(way, step + 1, h, slot).start()

    def finish_ring():
        for way in range(2):
            for step in range(4):
                for h in range(2):
                    if step > 0 or h == way:
                        hop(way, step, h, ring.at[way, step, h]).wait_send()

    closers.append(finish_ring)

    for h in range(2):
        total = part[h, y] + ring[0, 3, h] + ring[1, 3, h]
        for t in range(TILES):
            mine[ROWS * h:ROWS * (h + 1), t, :] = total[:, LANES * t:LANES * (t + 1)]

    def piece(k, source):
        peer = wrap(spot + k, SPOTS)
        return copy(
            mine.at[peer], pieces.at[source],
            piece_send.at[k], piece_recv.at[source], spot_device(peer),
        )

    each(1, SPOTS, lambda k: piece(k, spot).start())
    pltpu.make_async_copy(mine.at[spot], pieces.at[spot], piece_recv.at[spot]).start()
    each(0, SPOTS, lambda j: arrival(pieces.at[j], piece_recv.at[j]))
    closers.append(lambda: each(1, SPOTS, lambda k: piece(k, spot).wait_send()))
    done[me] = jnp.sum(pieces[...], axis=0) * (1.0 / CELLS)

    def give(k, source):
        peer = wrap(me + k, SPACE)
        return copy(
            done.at[me], done.at[source], out_send.at[k], out_recv.at[source], (peer, band)
        )

    each(1, SPACE, lambda k: give(k, me).start())
    each(EARLY, SPACE, lambda k: home_copy(k, me).start())
    closers.append(lambda: each(0, SPACE, lambda j: arrival(home_ref.at[j, pl.ds(away, 16)], home_recv.at[j])))
    closers.append(lambda: each(1, SPACE, lambda k: home_copy(k, me).wait_send()))
    each(1, SPACE, lambda k: give(k, wrap(me + k, SPACE)).wait_recv())
    closers.append(lambda: each(1, SPACE, lambda k: give(k, me).wait_send()))
    for t in range(TILES):
        margin_ref[:, LANES * t:LANES * (t + 1)] = done[:, t, :]

    for closer in closers:
        closer()


def shards(orbitals, potential):
    dma = pltpu.SemaphoreType.DMA
    f32 = jnp.float32
    vmem = pl.BlockSpec(memory_space=pltpu.VMEM)
    stay = pl.BlockSpec(memory_space=pl.ANY)
    padded = pltpu.VMEM((SPACE + 2, 32, LANES), f32)
    home, margin = pl.pallas_call(
        kernel,
        out_shape=(
            jax.ShapeDtypeStruct((ROWS, 32, LANES), f32),
            jax.ShapeDtypeStruct((ROWS, ORBS), f32),
        ),
        in_specs=[pl.BlockSpec(memory_space=pltpu.HBM)] * 2,
        out_specs=(stay, vmem),
        scratch_shapes=[
            padded, padded, padded,
            pltpu.VMEM((SPACE, 32, LANES), f32),
            pltpu.VMEM((SPACE, 32, LANES), f32),
            pltpu.VMEM((SPOTS, 16, LANES), f32),
            pltpu.VMEM((2, ORBS, LANES), f32),
            pltpu.VMEM((2 * N_Y, ROWS, 2 * LANES), f32),
            pltpu.VMEM((ORBS, 6 * LANES), jnp.bfloat16),
            pltpu.VMEM((2, N_Y, ROWS, ORBS), f32),
            pltpu.VMEM((2, 4, 2, ROWS, ORBS), f32),
            pltpu.VMEM((SPOTS, TILES, LANES), f32),
            pltpu.VMEM((SPOTS, TILES, LANES), f32),
            pltpu.VMEM((ROWS, TILES, LANES), f32),
            dma((SPACE,)), dma((SPACE,)), dma((SPACE,)), dma((SPACE,)),
            dma((2 * N_Y,)), dma((2 * N_Y,)), dma((2, SPOTS)), dma((2, SPOTS)),
            dma((2, 2, N_Y)), dma((2, 2, N_Y)), dma((2 * N_Y,)), dma((2 * N_Y,)),
            dma((SPACE,)), dma((SPACE,)),
            dma((2, 4, 2)), dma((2, 4, 2)), dma((SPOTS,)), dma((SPOTS,)), dma((SPACE,)), dma((SPACE,)), dma,
        ],
        compiler_params=pltpu.CompilerParams(
            collective_id=0, has_side_effects=True, vmem_limit_bytes=20 << 20
        ),
    )(
        orbitals.reshape(ROWS, 2, 16, LANES).transpose(0, 2, 1, 3).reshape(ROWS, 32, LANES),
        potential.reshape(2, 16, LANES).transpose(1, 0, 2).reshape(32, LANES),
    )
    filtered = home.reshape(ROWS, 16, 2, LANES).transpose(0, 2, 1, 3).reshape(ROWS, 2, 2048)
    return (filtered, margin)


def solution(mesh):
    return jax.shard_map(
        shards,
        mesh=mesh,
        in_specs=(P("band", "space", None), P("space", None)),
        out_specs=(P("band", "space", None), P("band", None)),
        check_vma=False,
    )
```

time: 114 us -> 111 us (0.974)
  Pallas kernels: 109 us -> 107 us
    pallas_call x1, Pallas kernels: 109 us -> 107 us  [shards(): pl.pallas_call(kernel, out_shape=(jax.ShapeDtypeStruct((ROWS, 32, LANES),...]
    unnamed x4 -> x6, local copies, waits for them, and re-layouts: 2.44 us -> 3.09 us
where the time goes in v4:
time: 111 us
  Pallas kernels  107 us (96%)
  local copies, waits for them, and re-layouts  3.09 us (3%)
    pallas_call x1, Pallas kernels, shards(): pl.pallas_call(kernel, out_shape=(jax.ShapeDtypeStruct((ROWS, 32, LANES),...  107 us
    unnamed x6, local copies, waits for them, and re-layouts  3.09 us

profile of v4, /device:TPU:1, one launch (start us, length us, event | category | flops | bytes accessed | tf_op | source)
XLA Modules:
  0.0 110.7 jit_solution(10356664956542207303)
XLA Ops:
  0.6 0.0 copy-start
  0.6 1.0 copy-done
  1.6 0.0 copy-start.1
  1.6 0.7 copy-done.1
  2.3 106.9 %shard_map.41 = (f32[24,32,128]{2,1,0:T(8,128)S(1)}, f32[24,768]{1,0:T(8,128)S(1)}) custom-call(f32[24,32,128]{2,1,0:T(8,128)S(1)} %bitcast.15, f32[32,128]{1,0:T(8,128)S(1)} %bitcast.17), custom_call_target="tpu_custom_call" | custom-call | tf_op jit(solution)/shard_map/pallas_call | solution.py:380
  109.3 0.7 copy.9
  110.0 0.6 copy.10
Async XLA Ops:
  0.6 1.0 copy-start
  1.6 0.7 copy-start.1

commit v5 on v4

--- a/solution.py
+++ b/solution.py
@@ -15,7 +15,6 @@
 LANES = 128
 TILES = ORBS // LANES
 CELLS = 48 * 2048
-EARLY = 24
 
 
 def kernel(
@@ -74,7 +73,8 @@
     def greet(peer):
         pl.semaphore_signal(barrier, inc=1, device_id=peer, device_id_type=MESH)
 
-    each(1, SPOTS, lambda k: greet(spot_device(wrap(spot + k, SPOTS))))
+    each(12, SPOTS, lambda k: greet(spot_device(wrap(spot + k, SPOTS))))
+    each(1, 12, lambda k: greet(spot_device(wrap(spot + k, SPOTS))))
     each(1, 2 * N_Y, lambda k: greet(seat_device(wrap(seat + k, 2 * N_Y))))
     pl.semaphore_wait(barrier, SPOTS - 1 + 2 * N_Y - 1)
 
@@ -270,7 +270,7 @@
             home_send.at[k], home_recv.at[orbital], (peer, band),
         )
 
-    each(1, EARLY, lambda k: home_copy(k, me).start())
+    homeward = iter(range(1, SPACE))
     near_copy = pltpu.make_async_copy(
         column.at[pl.ds(SPACE * z_hi, SPACE)], home_ref.at[:, pl.ds(near_rows, 16)], near_sem
     )
@@ -280,41 +280,48 @@
         last.at[me, pl.ds(away, 16)], home_ref.at[me, pl.ds(away, 16)], home_recv.at[me]
     ).start()
 
-    for g in range(2 * N_Y):
-        for k in range(2):
-            rows[g, :, LANES * k:LANES * (k + 1)] = held[
-                k, pl.ds(pl.multiple_of(ROWS * (2 * g + core), 8), ROWS), :
-            ]
-    left = rows[...].reshape(2 * N_Y * ROWS, 2 * LANES)
-    left_hi = left.astype(jnp.bfloat16)
-    left_lo = (left - left_hi.astype(jnp.float32)).astype(jnp.bfloat16)
-    left_cat = jnp.concatenate([left_hi, left_hi, left_lo], axis=1)
+    def hop(way, step, h, source):
+        return copy(
+            source, ring.at[way, step, h],
+            ring_send.at[way, step, h], ring_recv.at[way, step, h], up if way == 0 else down,
+        )
+
+    def goal(way, step):
+        return (4 - step if way == 0 else 4 + step) % N_Y
+
     for k in range(2):
         cells = held[k]
         cells_hi = cells.astype(jnp.bfloat16)
         cells_lo = (cells - cells_hi.astype(jnp.float32)).astype(jnp.bfloat16)
         for slot, value in enumerate((cells_hi, cells_lo, cells_hi)):
             cat[:, 2 * LANES * slot + LANES * k:2 * LANES * slot + LANES * (k + 1)] = value
-    for n in range(3):
-        block = lax.dot_general(
-            left_cat, cat[256 * n:256 * (n + 1), :], (((1,), (1,)), ((), ())),
-            preferred_element_type=jnp.float32,
-        )
-        part[:, :, :, 256 * n:256 * (n + 1)] = block.reshape(2, N_Y, ROWS, 256)
-
-    def hop(way, step, h, source):
-        return copy(
-            source, ring.at[way, step, h],
-            ring_send.at[way, step, h], ring_recv.at[way, step, h], up if way == 0 else down,
-        )
-
-    def goal(way, step):
-        return (y + (4 - step if way == 0 else 4 + step)) & 7
-
-    for way in range(2):
-        hop(way, 0, way, part.at[way, goal(way, 0)]).start()
-    for way in range(2):
-        hop(way, 1, 1 - way, part.at[1 - way, goal(way, 1)]).start()
+    for away_by in ((4, 3, 5), (2, 6, 1, 7, 0)):
+        groups = [(offset, h) for offset in away_by for h in range(2)]
+        for g, (offset, h) in enumerate(groups):
+            owner = 2 * (N_Y * h + ((y + offset) & 7)) + core
+            for k in range(2):
+                rows[g, :, LANES * k:LANES * (k + 1)] = held[
+                    k, pl.ds(pl.multiple_of(ROWS * owner, 8), ROWS), :
+                ]
+        left = rows[0:len(groups)].reshape(len(groups) * ROWS, 2 * LANES)
+        left_hi = left.astype(jnp.bfloat16)
+        left_lo = (left - left_hi.astype(jnp.float32)).astype(jnp.bfloat16)
+        left_cat = jnp.concatenate([left_hi, left_hi, left_lo], axis=1)
+        for n in range(3):
+            block = lax.dot_general(
+                left_cat, cat[256 * n:256 * (n + 1), :], (((1,), (1,)), ((), ())),
+                preferred_element_type=jnp.float32,
+            ).reshape(len(groups), ROWS, 256)
+            for g, (offset, h) in enumerate(groups):
+                part[h, offset, :, 256 * n:256 * (n + 1)] = block[g]
+        if 4 in away_by:
+            for way in range(2):
+                hop(way, 0, way, part.at[way, goal(way, 0)]).start()
+            for way in range(2):
+                hop(way, 1, 1 - way, part.at[1 - way, goal(way, 1)]).start()
+            for _ in range(3):
+                home_copy(next(homeward), me).start()
+
     for step in range(4):
         for turn in range(2 if step else 1):
             for way in range(2):
@@ -324,6 +331,10 @@
                 if step < 3:
                     ring[way, step, h] = ring[way, step, h] + part[h, goal(way, step + 1)]
                     hop(way, step + 1, h, slot).start()
+                    for _ in range(2):
+                        home_copy(next(homeward), me).start()
+
+    assert next(homeward, None) is None
 
     def finish_ring():
         for way in range(2):
@@ -335,7 +346,7 @@
     closers.append(finish_ring)
 
     for h in range(2):
-        total = part[h, y] + ring[0, 3, h] + ring[1, 3, h]
+        total = part[h, 0] + ring[0, 3, h] + ring[1, 3, h]
         for t in range(TILES):
             mine[ROWS * h:ROWS * (h + 1), t, :] = total[:, LANES * t:LANES * (t + 1)]
 
@@ -359,7 +370,6 @@
         )
 
     each(1, SPACE, lambda k: give(k, me).start())
-    each(EARLY, SPACE, lambda k: home_copy(k, me).start())
     closers.append(lambda: each(0, SPACE, lambda j: arrival(home_ref.at[j, pl.ds(away, 16)], home_recv.at[j])))
     closers.append(lambda: each(1, SPACE, lambda k: home_copy(k, me).wait_send()))
     each(1, SPACE, lambda k: give(k, wrap(me + k, SPACE)).wait_recv())
@@ -391,7 +401,7 @@
             pltpu.VMEM((SPACE, 32, LANES), f32),
             pltpu.VMEM((SPOTS, 16, LANES), f32),
             pltpu.VMEM((2, ORBS, LANES), f32),
-            pltpu.VMEM((2 * N_Y, ROWS, 2 * LANES), f32),
+            pltpu.VMEM((10, ROWS, 2 * LANES), f32),
             pltpu.VMEM((ORBS, 6 * LANES), jnp.bfloat16),
             pltpu.VMEM((2, N_Y, ROWS, ORBS), f32),
             pltpu.VMEM((2, 4, 2, ROWS, ORBS), f32),

time: 111 us -> 112 us (level)
  no operation moved by 1% of the time
where the time goes in v5:
time: 112 us; the launch traced here: 111 us
  Pallas kernels  108 us (96%)
  local copies, waits for them, and re-layouts  3.09 us (3%)
    pallas_call x1, Pallas kernels, shards(): pl.pallas_call(kernel, out_shape=(jax.ShapeDtypeStruct((ROWS, 32, LANES),...  108 us
    unnamed x6, local copies, waits for them, and re-layouts  3.09 us

profile of v5, /device:TPU:1, one launch (start us, length us, event | category | flops | bytes accessed | tf_op | source)
XLA Modules:
  0.0 111.4 jit_solution(8619981856335999465)
XLA Ops:
  0.6 0.0 copy-start
  0.6 1.0 copy-done
  1.6 0.0 copy-start.1
  1.6 0.7 copy-done.1
  2.3 107.7 %shard_map.41 = (f32[24,32,128]{2,1,0:T(8,128)S(1)}, f32[24,768]{1,0:T(8,128)S(1)}) custom-call(f32[24,32,128]{2,1,0:T(8,128)S(1)} %bitcast.15, f32[32,128]{1,0:T(8,128)S(1)} %bitcast.17), custom_call_target="tpu_custom_call" | custom-call | tf_op jit(solution)/shard_map/pallas_call | solution.py:390
  110.0 0.7 copy.9
  110.8 0.6 copy.10
Async XLA Ops:
  0.6 1.0 copy-start
  1.6 0.7 copy-start.1
